TPU v7x, 512 devices: a whole 4x8x8 slice. The times are simulated.
512 devices in a mesh: gx: 16 (over x, y_lo), gy: 32 (over z, y_hi, core).
Axes of the slice: x: 4, y: 8 (y_hi: 2, y_lo: 4; y = y_hi * 4 + y_lo), z: 8, core: 2. Of those that a mesh axis runs over, the one named last changes fastest.
Arguments:
- features: bfloat16 [16, 32, 1, 192, 512], P('gx', 'gy'), may hold values from -6 to 6
- occupancy: int32 [16, 32, 1, 512], P('gx', 'gy'), may hold values 0 or 1
- brick_pos: int32 [16, 32, 1], P('gx', 'gy'), may hold values from 0 to 3, as said below
- weight: bfloat16 [192, 27, 192], replicated, may hold values from -0.125 to 0.125
- cotangent: bfloat16 [16, 32, 1, 192, 512], P('gx', 'gy'), may hold values from -6 to 6
Outputs:
- output: bfloat16 [16, 32, 1, 192, 512], P('gx', 'gy')
- x_grad: bfloat16 [16, 32, 1, 192, 512], P('gx', 'gy')
- w_grad: float32 [192, 27, 192], P('gx', None, 'gy')
Inputs may be any that keep to these rules, and one draw needn't show every extreme that they name: `brick_pos`: the 1 positions of one device are distinct.
All inputs are finite; a program needn't handle non-finite values. No bound on the sum of `occupancy` on one device may be relied on, other than what follows from the above.
Results may differ from a plain program's by a relative error of at most 0.014.
Values may be sent and summed in bfloat16 or wider, within the bound.
A program may use at most 64 MiB of HBM per device.

v0:
```python
import jax
import jax.numpy as jnp
from jax import lax
from jax.sharding import PartitionSpec as P

BE = 8
TX = 2
TY = 2
HZ = 1


def extended(block, sides, width):
    for axis, dim in sides:
        count = lax.axis_size(axis)
        forward = [(i, i + 1) for i in range(count - 1)]
        backward = [(target, source) for source, target in forward]
        low = lax.ppermute(
            lax.slice_in_dim(block, block.shape[dim] - width, None, axis=dim), axis, forward
        )
        high = lax.ppermute(lax.slice_in_dim(block, 0, width, axis=dim), axis, backward)
        block = jnp.concatenate([low, block, high], axis=dim)
    return block


def silu_slope(values_in):
    sigma = jax.nn.sigmoid(values_in)
    return sigma * (1.0 + values_in * (1.0 - sigma))


def tap_columns(window):
    channels = window.shape[3]
    pieces = []
    for tap_x in range(3):
        for tap_y in range(3):
            for tap_z in range(3):
                start_x, start_y, start_z = (2 - tap_x, 2 - tap_y, 2 - tap_z)
                piece_view = window[
                    start_x : start_x + BE, start_y : start_y + BE, start_z : start_z + BE, :
                ]
                pieces.append(piece_view.reshape(BE * BE * BE, channels))
    return jnp.concatenate(pieces, axis=1)


def corner_starts(positions):
    start_x = positions // (TY * HZ) * BE
    start_y = positions // HZ % TY * BE
    start_z = positions % HZ * BE
    return (start_x, start_y, start_z)


def cut_cube(lattice, starts, slot_id, edge_len):
    zero_idx = jnp.zeros((), jnp.int32)
    return lax.dynamic_slice(
        lattice,
        (starts[0][slot_id], starts[1][slot_id], starts[2][slot_id], zero_idx),
        (edge_len, edge_len, edge_len, lattice.shape[3]),
    )


def place_bricks(bricks, starts):
    slot_count, channels = (bricks.shape[0], bricks.shape[2])
    lattice = jnp.zeros((TX * BE, TY * BE, HZ * BE, channels), bricks.dtype)
    zero_idx = jnp.zeros((), jnp.int32)
    cube_part = bricks[0].reshape(BE, BE, BE, channels)
    lattice = lax.dynamic_update_slice(
        lattice, cube_part, (starts[0][0], starts[1][0], starts[2][0], zero_idx)
    )
    return lattice


def fold_rims(padded, outer_cycle):
    inner_sum = padded[1:-1, 1:-1, 1:-1, :]
    rim_cycle = outer_cycle[:, :, 1:-1, :]
    inner_sum = inner_sum.at[0, :, :, :].add(rim_cycle[0, 2:-2])
    inner_sum = inner_sum.at[-1, :, :, :].add(rim_cycle[-1, 2:-2])
    inner_sum = inner_sum.at[:, 0, :, :].add(rim_cycle[2:-2, 0])
    inner_sum = inner_sum.at[:, -1, :, :].add(rim_cycle[2:-2, -1])
    inner_sum = inner_sum.at[0, 0, :, :].add(rim_cycle[0, 0])
    inner_sum = inner_sum.at[0, -1, :, :].add(rim_cycle[0, -1])
    inner_sum = inner_sum.at[-1, 0, :, :].add(rim_cycle[-1, 0])
    inner_sum = inner_sum.at[-1, -1, :, :].add(rim_cycle[-1, -1])
    return inner_sum


def shards(features, occupancy, brick_pos, weight, cotangent):
    bricks = features[0, 0].transpose(0, 2, 1)
    slot_count, voxels, channels = bricks.shape
    live_mask = occupancy[0, 0].astype(jnp.bfloat16)[:, :, None]
    starts = corner_starts(brick_pos[0, 0])
    masked = bricks * live_mask
    zero_idx = jnp.zeros((), jnp.int32)
    tap_weight = weight.transpose(1, 0, 2).reshape(27 * channels, channels)
    padded = jnp.zeros((TX * BE + 2, TY * BE + 2, HZ * BE + 2, channels), jnp.float32)
    slot_id = 0
    tap_terms = jnp.einsum(
        "vi,ki->vk", masked[slot_id], tap_weight, preferred_element_type=jnp.float32
    ).reshape(BE, BE, BE, 27, channels)
    spread = jnp.zeros((BE + 2, BE + 2, BE + 2, channels), jnp.float32)
    for tap_x in range(3):
        for tap_y in range(3):
            for tap_z in range(3):
                tap_id = 9 * tap_x + 3 * tap_y + tap_z
                spread = spread.at[
                    2 - tap_x : 2 - tap_x + BE,
                    2 - tap_y : 2 - tap_y + BE,
                    2 - tap_z : 2 - tap_z + BE,
                    :,
                ].add(tap_terms[:, :, :, tap_id, :])
    padded = lax.dynamic_update_slice(
        padded, spread, (starts[0][slot_id], starts[1][slot_id], starts[2][slot_id], zero_idx)
    )
    outer_cycle = extended(padded.astype(jnp.bfloat16), (("gx", 0), ("gy", 1)), 1).astype(
        padded.dtype
    )
    folded = fold_rims(padded, outer_cycle)
    slot_id = 0
    pre_list = [cut_cube(folded, starts, slot_id, BE).reshape(voxels, channels)]
    pre_act = jnp.stack(pre_list, axis=0)
    output = (jax.nn.silu(pre_act) * live_mask).astype(jnp.bfloat16)
    cot_last = cotangent[0, 0].transpose(0, 2, 1)
    slope = (cot_last.astype(jnp.float32) * silu_slope(pre_act) * live_mask).astype(jnp.bfloat16)
    grad_lattice = place_bricks(slope, starts)
    grad_wide = extended(grad_lattice, (("gx", 0), ("gy", 1)), 1)
    grad_wide = jnp.pad(grad_wide, ((0, 0), (0, 0), (1, 1), (0, 0)))
    slot_id = 0
    window = cut_cube(grad_wide, starts, slot_id, BE + 2)
    columns = tap_columns(window)
    back_grad = jnp.dot(columns, tap_weight, preferred_element_type=jnp.float32)
    back_list = [(back_grad * live_mask[slot_id]).astype(jnp.bfloat16)]
    tap_sum = jnp.einsum("vk,vi->ki", columns, masked[slot_id], preferred_element_type=jnp.float32)
    x_grad = jnp.stack(back_list, axis=0).transpose(0, 2, 1)
    weight_sum = tap_sum.reshape(27, channels, channels).transpose(1, 0, 2)
    total_bricks = slot_count * lax.axis_size("gx") * lax.axis_size("gy")
    summed = lax.psum(weight_sum, ("gx", "gy"))
    row_count = channels // lax.axis_size("gx")
    col_count = channels // lax.axis_size("gy")
    own_share = lax.dynamic_slice(
        summed,
        (lax.axis_index("gx") * row_count, zero_idx, lax.axis_index("gy") * col_count),
        (row_count, 27, col_count),
    )
    w_grad = own_share / total_bricks
    return (output.transpose(0, 2, 1)[None, None], x_grad[None, None], w_grad)


def solution(mesh):
    placed = (
        P("gx", "gy", None, None, None),
        P("gx", "gy", None, None),
        P("gx", "gy", None),
        P(),
        P("gx", "gy", None, None, None),
    )
    return jax.shard_map(
        shards,
        mesh=mesh,
        in_specs=placed,
        out_specs=(
            P("gx", "gy", None, None, None),
            P("gx", "gy", None, None, None),
            P("gx", None, "gy"),
        ),
        check_vma=False,
    )
```

profile of v0, /device:TPU:57, one launch (start us, length us, event | category | flops | bytes accessed | tf_op | source)
XLA Modules:
  0.0 555.9 jit_solution(4422146013753918328)
XLA Ops:
  12.1 5.0 copy-done.4
  19.4 4.1 scatter-add.119
  25.6 2.3 fusion.45
  27.9 4.2 scatter-add.121
  32.1 2.3 fusion.44
  34.4 4.2 scatter-add.124
  40.6 2.3 fusion.41
  42.9 4.2 scatter-add.126
  47.1 2.3 fusion.40
  49.4 4.2 scatter-add.129
  55.7 2.3 fusion.37
  58.0 4.2 scatter-add.131
  62.1 2.3 fusion.36
  64.4 4.2 scatter-add.134
  70.7 2.3 fusion.33
  72.9 4.2 scatter-add.136
  77.1 2.3 fusion.32
  79.4 4.2 scatter-add.139
  85.8 2.3 fusion.29
  88.0 4.2 scatter-add.141
  92.2 2.3 fusion.28
  94.5 4.2 scatter-add.144
  100.8 2.3 fusion.25
  103.1 4.2 scatter-add.146
  107.3 2.3 fusion.24
  109.5 4.2 scatter-add.149
  116.4 4.2 fusion.21
  120.7 6.1 %scatter-add.151 = f32[10,10,10,192]{3,2,1,0:T(8,128)} dynamic-update-slice(f32[10,10,10,192]{3,2,1,0:T(8,128)} %fusion.23, f32[8,8,8,192]{3,2,1,0:T(8,128)} %fusion.21, s32[]{:T(128)} %bitcast.29, s32[]{:T(128)} %bitcast.30, s32[]{:T(128)} %bitcast.31, s32[]{:T(128)} %constant.1171.clone.1) | dynamic-update-slice | bytes 786436 | tf_op jit(solution)/shard_map/scatter-add | solution.py:108
  126.8 2.3 fusion.20
  129.1 4.2 scatter-add.154
  137.7 4.2 scatter-add.156
  141.8 2.3 fusion.16
  144.1 4.2 scatter-add.159
  153.6 5.5 collective-permute-start
  164.7 3.7 collective-permute-done.1
  169.4 5.2 collective-permute-start.2
  178.6 9.2 %collective-permute-done.3 = bf16[20,1,10,192]{3,2,1,0:T(8,128)(2,1)S(1)} collective-permute-done((bf16[20,1,10,192]{3,2,1,0:T(8,128)(2,1)S(1)}, bf16[20,1,10,192]{3,2,1,0:T(8,128)(2,1)S(1)}, u32[]{:S(2)}, u32[]{:S(2)}) %collective-permute-start.3) | collective-permute-done | bytes 76832 | tf_op jit(solution)/shard_map/ppermute | solution.py:20
  195.7 3.2 fusion.58
  205.6 3.4 collective-permute-start.5
  208.9 4.3 collective-permute-done.5
  213.3 2.7 collective-permute-start.6
  218.7 7.8 %collective-permute-done.7 = bf16[18,1,8,192]{3,2,1,0:T(8,128)(2,1)S(1)} collective-permute-done((bf16[18,1,8,192]{3,2,1,0:T(8,128)(2,1)S(1)}, bf16[18,1,8,192]{3,2,1,0:T(8,128)(2,1)S(1)}, u32[]{:S(2)}, u32[]{:S(2)}) %collective-permute-start.7) | collective-permute-done | bytes 55328 | tf_op jit(solution)/shard_map/ppermute | solution.py:20
  227.7 2.4 fusion.64
  231.6 10.1 %concatenate.141 = bf16[512,5184]{1,0:T(8,128)(2,1)} concatenate(bf16[512,192]{1,0:T(8,128)(2,1)} %bitcast.301, bf16[512,192]{1,0:T(8,128)(2,1)} %bitcast.300, bf16[512,192]{1,0:T(8,128)(2,1)} %bitcast.299, bf16[512,192]{1,0:T(8,128)(2,1)} %bitcast.298, bf16[512,192]{1,0:T(8,128)(2,1)} %bitcast.297, bf16[512,192]{1,0:T(8,128)(2,1)} %bitcast.296, bf16[512,192]{1,0:T(8,128)(2,1)} %bitcast.295, ...), dimensions={1} | concatenate | bytes 10616832 | tf_op jit(solution)/shard_map/concatenate | solution.py:41
  241.7 8.1 %copy.65 = bf16[5184,512]{1,0:T(8,128)(2,1)} copy(bf16[5184,512]{0,1:T(8,128)(2,1)} %bitcast.271) | data formatting | bytes 10616832 | tf_op jit(solution)/shard_map/vk,vi->ki/dot_general | solution.py:130
  249.8 6.4 %convolution_bitcast_fusion = f32[192,27,192]{2,0,1:T(8,128)} fusion(bf16[27,192,512]{2,1,0:T(8,128)(2,1)} %bitcast.272, bf16[1,192,512]{1,2,0:T(8,128)(2,1)S(1)} %bitcast_multiply_fusion), kind=kOutput, calls=%fused_computation.11 | convolution fusion | flops 1019215872 | bytes 9486336 | tf_op jit(solution)/shard_map/vk,vi->ki/dot_general | solution.py:130
  258.0 5.1 fusion.4
  263.1 284.0 %all-reduce.4.cloned.1.call-done = f32[192,27,192]{2,0,1:T(8,128)} async-done(((f32[192,27,192]{2,0,1:T(8,128)}), f32[192,27,192]{2,0,1:T(8,128)}) %all-reduce.4.cloned.1.call-update) | async-done | bytes 3981328 | tf_op jit(solution)/shard_map/psum | solution.py:134
  (74 shorter events, 65.5 us)
Async XLA Ops:
  7.2 2.8 copy-start
  7.2 539.9 %all-reduce.4.cloned.1.call-start = ((), (), s32[]{:S(2)}) async-start(), calls=%async_computation | async-start | bytes 10616832 | tf_op jit(solution)/shard_map/psum | solution.py:134
  12.0 5.1 copy-start.4
  150.4 1.4 copy-start.3
  152.0 9.2 %copy-start.5 = (f32[18,18,10,192]{3,2,1,0:T(8,128)}, f32[18,18,10,192]{3,2,1,0:T(8,128)S(1)}, u32[]{:S(2)}) copy-start(f32[18,18,10,192]{3,2,1,0:T(8,128)S(1)} %constant_dynamic-update-slice_fusion.1) | copy-start | bytes 7464964
  152.4 10.4 %copy-start.1 = (bf16[18,18,10,192]{3,2,1,0:T(8,128)(2,1)}, bf16[18,18,10,192]{3,2,1,0:T(8,128)(2,1)S(1)}, u32[]{:S(2)}) copy-start(bf16[18,18,10,192]{3,2,1,0:T(8,128)(2,1)S(1)} %convert_element_type.72) | copy-start | bytes 3732484
  153.6 11.1 %collective-permute-start = (bf16[1,18,10,192]{3,2,1,0:T(8,128)(2,1)}, bf16[1,18,10,192]{3,2,1,0:T(8,128)(2,1)S(1)}, u32[]{:S(2)}, u32[]{:S(2)}) collective-permute-start(bf16[1,18,10,192]{3,2,1,0:T(8,128)(2,1)} %get-tuple-element.431), channel_id=1, source_target_pairs={{0,32},{32,64},{64,96},{96,128},{128,160},{160,192},{192,224},{224... | collective-permute-start | bytes 207368 | tf_op jit(solution)/shard_map/ppermute | solution.py:17
  159.1 4.9 copy-start.7
  159.1 9.3 %collective-permute-start.1 = (bf16[1,18,10,192]{3,2,1,0:T(8,128)(2,1)}, bf16[1,18,10,192]{3,2,1,0:T(8,128)(2,1)S(1)}, u32[]{:S(2)}, u32[]{:S(2)}) collective-permute-start(bf16[1,18,10,192]{3,2,1,0:T(8,128)(2,1)} %get-tuple-element.432), channel_id=1, source_target_pairs={{32,0},{64,32},{96,64},{128,96},{160,128},{192,160},{224,192},{256... | collective-permute-start | bytes 207368 | tf_op jit(solution)/shard_map/ppermute | solution.py:20
  163.9 24.0 %copy-start.2 = (bf16[18,18,10,192]{3,2,1,0:T(8,128)(2,1)S(1)}, bf16[18,18,10,192]{3,2,1,0:T(8,128)(2,1)}, u32[]{:S(2)}) copy-start(bf16[18,18,10,192]{3,2,1,0:T(8,128)(2,1)} %copy-done.1) | copy-start | bytes 3732484
  169.4 9.2 %collective-permute-start.2 = (bf16[20,1,10,192]{3,2,1,0:T(8,128)(2,1)S(1)}, bf16[20,1,10,192]{3,2,1,0:T(8,128)(2,1)S(1)}, u32[]{:S(2)}, u32[]{:S(2)}) collective-permute-start(bf16[20,1,10,192]{3,2,1,0:T(8,128)(2,1)S(1)} %get-tuple-element.429), channel_id=1, source_target_pairs={{0,1},{1,2},{2,3},{3,4},{4,5},{5,6},{6,7},{7,8},{8,9},{9,10},{10,1... | collective-permute-start | bytes 230408 | tf_op jit(solution)/shard_map/ppermute | solution.py:17
  174.6 13.2 %collective-permute-start.3 = (bf16[20,1,10,192]{3,2,1,0:T(8,128)(2,1)S(1)}, bf16[20,1,10,192]{3,2,1,0:T(8,128)(2,1)S(1)}, u32[]{:S(2)}, u32[]{:S(2)}) collective-permute-start(bf16[20,1,10,192]{3,2,1,0:T(8,128)(2,1)S(1)} %get-tuple-element.430), channel_id=1, source_target_pairs={{1,0},{2,1},{3,2},{4,3},{5,4},{6,5},{7,6},{8,7},{9,8},{10,9},{11,1... | collective-permute-start | bytes 230408 | tf_op jit(solution)/shard_map/ppermute | solution.py:20
  203.6 5.3 collective-permute-start.4
  205.6 7.7 %collective-permute-start.5 = (bf16[1,16,8,192]{3,2,1,0:T(8,128)(2,1)S(1)}, bf16[1,16,8,192]{3,2,1,0:T(8,128)(2,1)S(1)}, u32[]{:S(2)}, u32[]{:S(2)}) collective-permute-start(bf16[1,16,8,192]{3,2,1,0:T(8,128)(2,1)S(1)} %get-tuple-element.435), channel_id=1, source_target_pairs={{32,0},{64,32},{96,64},{128,96},{160,128},{192,160},{224,192},{256... | collective-permute-start | bytes 147464 | tf_op jit(solution)/shard_map/ppermute | solution.py:20
  213.3 5.4 collective-permute-start.6
  216.0 10.5 %collective-permute-start.7 = (bf16[18,1,8,192]{3,2,1,0:T(8,128)(2,1)S(1)}, bf16[18,1,8,192]{3,2,1,0:T(8,128)(2,1)S(1)}, u32[]{:S(2)}, u32[]{:S(2)}) collective-permute-start(bf16[18,1,8,192]{3,2,1,0:T(8,128)(2,1)S(1)} %get-tuple-element.433), channel_id=1, source_target_pairs={{1,0},{2,1},{3,2},{4,3},{5,4},{6,5},{7,6},{8,7},{9,8},{10,9},{11,1... | collective-permute-start | bytes 165896 | tf_op jit(solution)/shard_map/ppermute | solution.py:20
  256.2 0.9 copy-start.6
Sparse Core Ops, SparseCore 0:
  256.4 290.6 all-reduce.3
where the time goes:
time: 562 us; the launch traced here: 556 us
  waiting for transfers between devices  311 us (55%)
  local copies, waits for them, and re-layouts  113 us (20%)
  other arithmetic  79.2 us (14%)
  starting transfers between devices  24.7 us (4%)
  between operations  15.2 us (3%)
  matrix products  13.6 us (2%)
    psum x1, waiting for transfers between devices, shards(): summed = lax.psum(weight_sum, ('gx', 'gy'))  284 us
    scatter-add x18, local copies, waits for them, and re-layouts, shards(): spread = spread.at[2 - tap_x:2 - tap_x + BE, 2 - tap_y:2 - tap_y + BE, 2...  74.3 us
    add x17, other arithmetic, shards(): spread = spread.at[2 - tap_x:2 - tap_x + BE, 2 - tap_y:2 - tap_y + BE, 2...  39.5 us
    ppermute x4, waiting for transfers between devices, extended(): lax.ppermute(lax.slice_in_dim(block, 0, width, axis=dim), axis, backward)  25.1 us
    scatter-add x9, other arithmetic, shards(): spread = spread.at[2 - tap_x:2 - tap_x + BE, 2 - tap_y:2 - tap_y + BE, 2...  19 us
    ppermute x4, starting transfers between devices, extended(): lax.ppermute(lax.slice_in_dim(block, block.shape[dim] - width, None, axis...  15.4 us
  transfers between devices with their start and end apart: 9, of which 6 were waited for; matrix products, arithmetic and copies ran while one was open for 2% of the time, Pallas kernels for 0%

commit v1 on v0

v1 whole, which is shorter than its diff:
```python
import jax
import jax.numpy as jnp
from jax import lax
from jax.sharding import PartitionSpec as P

BE = 8
TX = 2
TY = 2


def extended(block, sides, width):
    for axis, dim in sides:
        count = lax.axis_size(axis)
        forward = [(i, i + 1) for i in range(count - 1)]
        backward = [(target, source) for source, target in forward]
        low = lax.ppermute(
            lax.slice_in_dim(block, block.shape[dim] - width, None, axis=dim), axis, forward
        )
        high = lax.ppermute(lax.slice_in_dim(block, 0, width, axis=dim), axis, backward)
        block = jnp.concatenate([low, block, high], axis=dim)
    return block


def silu_slope(v):
    sigma = jax.nn.sigmoid(v)
    return sigma * (1.0 + v * (1.0 - sigma))


def columns_of(bricks, start, flip):
    channels = bricks.shape[1]
    cube = bricks.reshape(BE, BE, BE, channels)
    zero = jnp.zeros((), jnp.int32)
    lattice = jnp.zeros((TX * BE, TY * BE, BE, channels), bricks.dtype)
    lattice = lax.dynamic_update_slice(lattice, cube, (start[0], start[1], zero, zero))
    wide = extended(lattice, (("gx", 0), ("gy", 1)), 1)
    window = lax.dynamic_slice(
        wide, (start[0], start[1], zero, zero), (BE + 2, BE + 2, BE, channels)
    )
    window = jnp.pad(window, ((0, 0), (0, 0), (1, 1), (0, 0)))
    pieces = []
    for a in range(3):
        for b in range(3):
            for c in range(3):
                s = (2 - a, 2 - b, 2 - c) if flip else (a, b, c)
                view = window[s[0] : s[0] + BE, s[1] : s[1] + BE, s[2] : s[2] + BE, :]
                pieces.append(view.reshape(BE * BE * BE, channels))
    return jnp.concatenate(pieces, axis=1)


def shards(features, occupancy, brick_pos, weight, cotangent):
    x = features[0, 0, 0]
    channels, voxels = x.shape
    mask = occupancy[0, 0].astype(jnp.bfloat16)
    pos = brick_pos[0, 0, 0]
    start = (pos // TY * BE, pos % TY * BE)
    xm = (x * mask).T
    cols = columns_of(xm, start, False)
    w_fwd = weight.reshape(channels, 27 * channels)
    pre = jnp.einsum("ok,vk->ov", w_fwd, cols, preferred_element_type=jnp.float32)
    maskf = mask.astype(jnp.float32)
    output = (jax.nn.silu(pre) * maskf).astype(jnp.bfloat16)
    g = (cotangent[0, 0, 0].astype(jnp.float32) * silu_slope(pre) * maskf).astype(jnp.bfloat16)
    wsum = jnp.einsum("ov,vk->ok", g, cols, preferred_element_type=jnp.float32)
    gcols = columns_of(g.T, start, True)
    w_bwd = weight.transpose(1, 0, 2).reshape(27 * channels, channels)
    back = jnp.einsum("ki,vk->iv", w_bwd, gcols, preferred_element_type=jnp.float32)
    x_grad = (back * maskf).astype(jnp.bfloat16)
    nx, ny = lax.axis_size("gx"), lax.axis_size("gy")
    rows, colw = channels // nx, channels // ny
    part = wsum.astype(jnp.bfloat16).reshape(nx, rows, 27 * channels)
    part = lax.all_to_all(part, "gx", 0, 0)
    part = part.astype(jnp.float32).sum(0)
    part = part.reshape(rows * 27, ny, colw).transpose(1, 0, 2).reshape(ny, rows * 27 * colw)
    part = lax.all_to_all(part.astype(jnp.bfloat16), "gy", 0, 0)
    part = part.astype(jnp.float32).sum(0)
    w_grad = part.reshape(rows, 27, colw) / (nx * ny)
    return (output[None, None, None], x_grad[None, None, None], w_grad)


def solution(mesh):
    placed = (
        P("gx", "gy", None, None, None),
        P("gx", "gy", None, None),
        P("gx", "gy", None),
        P(),
        P("gx", "gy", None, None, None),
    )
    return jax.shard_map(
        shards,
        mesh=mesh,
        in_specs=placed,
        out_specs=(
            P("gx", "gy", None, None, None),
            P("gx", "gy", None, None, None),
            P("gx", None, "gy"),
        ),
        check_vma=False,
    )
```

time: 562 us -> 204 us (0.36)
  the two profiles are of different devices: /device:TPU:57 before, /device:TPU:11 now
where the time goes in v1:
time: 204 us; the launch traced here: 202 us
  waiting for transfers between devices  74.8 us (37%)
  starting transfers between devices  59 us (29%)
  local copies, waits for them, and re-layouts  49 us (24%)
  matrix products  11.8 us (6%)
  other arithmetic  5.24 us (3%)
    ppermute x4, waiting for transfers between devices, extended(): lax.ppermute(lax.slice_in_dim(block, block.shape[dim] - width, None, axis...  51.6 us
    ppermute x4, starting transfers between devices, extended(): lax.ppermute(lax.slice_in_dim(block, block.shape[dim] - width, None, axis...  28.8 us
    concatenate x2, local copies, waits for them, and re-layouts, columns_of(): return jnp.concatenate(pieces, axis=1)  20 us
    ppermute x4, waiting for transfers between devices, extended(): lax.ppermute(lax.slice_in_dim(block, 0, width, axis=dim), axis, backward)  16 us
    convert_element_type x4, local copies, waits for them, and re-layouts, shards(): part = lax.all_to_all(part.astype(jnp.bfloat16), 'gy', 0, 0)  12.2 us
    all_to_all x1, starting transfers between devices, shards(): part = lax.all_to_all(part.astype(jnp.bfloat16), 'gy', 0, 0)  11.6 us
    all_to_all x1, starting transfers between devices, shards(): part = lax.all_to_all(part, 'gx', 0, 0)  10.3 us
    ppermute x4, starting transfers between devices, extended(): lax.ppermute(lax.slice_in_dim(block, 0, width, axis=dim), axis, backward)  8.29 us
  transfers between devices with their start and end apart: 10, of which 6 were waited for; matrix products, arithmetic and copies ran while one was open for 11% of the time, Pallas kernels for 0%

profile of v1, /device:TPU:11, one launch (start us, length us, event | category | flops | bytes accessed | tf_op | source)
XLA Modules:
  0.0 201.6 jit_solution(6274905942035821307)
XLA Ops:
  0.6 0.0 copy-start.1
  1.5 0.7 convert_reduce_fusion.1
  2.2 1.1 copy.13
  3.2 0.1 bitcast_multiply_fusion
  3.4 0.1 broadcast.16.clone
  3.6 3.2 %collective-permute-start = (bf16[1,16,8,192]{3,2,1,0:T(8,128)(2,1)S(1)}, bf16[1,16,8,192]{3,2,1,0:T(8,128)(2,1)S(1)}, u32[]{:S(2)}, u32[]{:S(2)}) collective-permute-start(bf16[1,16,8,192]{3,2,1,0:T(8,128)(2,1)S(1)} %get-tuple-element.15), channel_id=1, source_target_pairs={{0,32},{32,64},{64,96},{96,128},{128,160},{160,192},{192,224},{224... | collective-permute-start | bytes 147464 | tf_op jit(solution)/shard_map/ppermute | solution.py:16
  6.8 2.1 %collective-permute-start.1 = (bf16[1,16,8,192]{3,2,1,0:T(8,128)(2,1)S(1)}, bf16[1,16,8,192]{3,2,1,0:T(8,128)(2,1)S(1)}, u32[]{:S(2)}, u32[]{:S(2)}) collective-permute-start(bf16[1,16,8,192]{3,2,1,0:T(8,128)(2,1)S(1)} %get-tuple-element.16), channel_id=1, source_target_pairs={{32,0},{64,32},{96,64},{128,96},{160,128},{192,160},{224,192},{256... | collective-permute-start | bytes 147464 | tf_op jit(solution)/shard_map/ppermute | solution.py:19
  8.9 3.3 %collective-permute-done.1 = bf16[1,16,8,192]{3,2,1,0:T(8,128)(2,1)S(1)} collective-permute-done((bf16[1,16,8,192]{3,2,1,0:T(8,128)(2,1)S(1)}, bf16[1,16,8,192]{3,2,1,0:T(8,128)(2,1)S(1)}, u32[]{:S(2)}, u32[]{:S(2)}) %collective-permute-start.1) | collective-permute-done | bytes 49184 | tf_op jit(solution)/shard_map/ppermute | solution.py:19
  12.2 8.0 %collective-permute-start.2 = (bf16[18,1,8,192]{3,2,1,0:T(8,128)(2,1)S(1)}, bf16[18,1,8,192]{3,2,1,0:T(8,128)(2,1)S(1)}, u32[]{:S(2)}, u32[]{:S(2)}) collective-permute-start(bf16[18,1,8,192]{3,2,1,0:T(8,128)(2,1)S(1)} %get-tuple-element.12), channel_id=1, source_target_pairs={{0,1},{1,2},{2,3},{3,4},{4,5},{5,6},{6,7},{7,8},{8,9},{9,10},{10,1... | collective-permute-start | bytes 165896 | tf_op jit(solution)/shard_map/ppermute | solution.py:16
  20.2 1.9 collective-permute-start.3
  22.1 3.4 %copy.14 = bf16[192,27,192]{0,2,1:T(8,128)(2,1)} copy(bf16[192,27,192]{2,0,1:T(8,128)(2,1)S(1)} %copy-done.1) | data formatting | bytes 3981312 | tf_op args[3]
  25.5 4.2 %collective-permute-done.3 = bf16[18,1,8,192]{3,2,1,0:T(8,128)(2,1)S(1)} collective-permute-done((bf16[18,1,8,192]{3,2,1,0:T(8,128)(2,1)S(1)}, bf16[18,1,8,192]{3,2,1,0:T(8,128)(2,1)S(1)}, u32[]{:S(2)}, u32[]{:S(2)}) %collective-permute-start.3) | collective-permute-done | bytes 55328 | tf_op jit(solution)/shard_map/ppermute | solution.py:19
  29.8 1.2 fusion.7
  31.0 2.4 %pad_slice_fusion.18 = (bf16[8,8,8,192]{3,2,1,0:T(8,128)(2,1)S(1)}, bf16[8,8,8,192]{3,2,1,0:T(8,128)(2,1)S(1)}, bf16[8,8,8,192]{3,2,1,0:T(8,128)(2,1)S(1)}, bf16...) fusion(bf16[10,10,8,192]{3,2,1,0:T(8,128)(2,1)S(1)} %fusion.7), kind=kLoop, calls=%fused_computation.19 | loop fusion | bytes 4669440 | tf_op jit(solution)/shard_map/slice | solution.py:45
  33.4 1.4 fusion.16
  34.8 10.1 %concatenate.20 = bf16[512,5184]{1,0:T(8,128)(2,1)} concatenate(bf16[512,192]{1,0:T(8,128)(2,1)} %bitcast.130, bf16[512,192]{1,0:T(8,128)(2,1)} %bitcast.129, bf16[512,192]{1,0:T(8,128)(2,1)S(1)} %bitcast.97, bf16[512,192]{1,0:T(8,128)(2,1)S(1)} %bitcast.98, bf16[512,192]{1,0:T(8,128)(2,1)} %bitcast.128, bf16[512,192]{1,0:T(8,128)(2,1)} %bitcast.99, bf16[512,192]{1,0:T(8,128)(2,1)} %bitcast.100, ...), dimensions={1} | concatenate | bytes 10616832 | tf_op jit(solution)/shard_map/concatenate | solution.py:47
  44.9 5.4 %fusion.11 = (bf16[192,512]{1,0:T(8,128)(2,1)S(1)}, bf16[1,1,1,192,512]{4,3,2,1,0:T(8,128)(2,1)}) fusion(bf16[1,1,1,192,512]{4,3,2,1,0:T(8,128)(2,1)} %param.9, f32[512]{0:T(512)S(1)} %convert_element_type.70, bf16[512,5184]{1,0:T(8,128)(2,1)} %concatenate.20, bf16[192,5184]{0,1:T(8,128)(2,1)S(1)} %bitcast.94), kind=kOutput, calls=%fused_computation.61 | convolution fusion | flops 1020592128 | bytes 7890944 | tf_op jit(solution)/shard_map/ok,vk->ov/dot_general | solution.py:59
  50.4 1.2 convolution_convert_fusion
  51.6 2.2 %reshape.276 = bf16[16,12,5184]{2,1,0:T(8,128)(2,1)} reshape(bf16[192,5184]{1,0:T(8,128)(2,1)S(1)} %convolution_convert_fusion) | data formatting | bytes 3981312 | tf_op jit(solution)/shard_map/reshape | solution.py:70
  53.9 10.3 %all-to-all-start = ((bf16[16,12,5184]{2,1,0:T(8,128)(2,1)}), bf16[16,12,5184]{2,1,0:T(8,128)(2,1)S(1)}, u32[]{:S(2)}, u32[]{:S(2)}) async-start(bf16[16,12,5184]{2,1,0:T(8,128)(2,1)} %reshape.276), calls=%async_computation | async-start | bytes 5373952 | tf_op jit(solution)/shard_map/all_to_all | solution.py:71
  64.2 0.1 copy.15
  64.3 0.1 broadcast.16
  64.5 3.1 %collective-permute-start.4 = (bf16[1,16,8,192]{3,2,1,0:T(8,128)(2,1)S(1)}, bf16[1,16,8,192]{3,2,1,0:T(8,128)(2,1)S(1)}, u32[]{:S(2)}, u32[]{:S(2)}) collective-permute-start(bf16[1,16,8,192]{3,2,1,0:T(8,128)(2,1)S(1)} %get-tuple-element.13), channel_id=1, source_target_pairs={{0,32},{32,64},{64,96},{96,128},{128,160},{160,192},{192,224},{224... | collective-permute-start | bytes 147464 | tf_op jit(solution)/shard_map/ppermute | solution.py:16
  67.6 2.2 %collective-permute-start.5 = (bf16[1,16,8,192]{3,2,1,0:T(8,128)(2,1)S(1)}, bf16[1,16,8,192]{3,2,1,0:T(8,128)(2,1)S(1)}, u32[]{:S(2)}, u32[]{:S(2)}) collective-permute-start(bf16[1,16,8,192]{3,2,1,0:T(8,128)(2,1)S(1)} %get-tuple-element.14), channel_id=1, source_target_pairs={{32,0},{64,32},{96,64},{128,96},{160,128},{192,160},{224,192},{256... | collective-permute-start | bytes 147464 | tf_op jit(solution)/shard_map/ppermute | solution.py:19
  69.8 51.6 %collective-permute-done.4 = bf16[1,16,8,192]{3,2,1,0:T(8,128)(2,1)S(1)} collective-permute-done((bf16[1,16,8,192]{3,2,1,0:T(8,128)(2,1)S(1)}, bf16[1,16,8,192]{3,2,1,0:T(8,128)(2,1)S(1)}, u32[]{:S(2)}, u32[]{:S(2)}) %collective-permute-start.4) | collective-permute-done | bytes 49184 | tf_op jit(solution)/shard_map/ppermute | solution.py:16
  121.3 1.1 collective-permute-done.5
  122.4 14.4 %collective-permute-start.6 = (bf16[18,1,8,192]{3,2,1,0:T(8,128)(2,1)S(1)}, bf16[18,1,8,192]{3,2,1,0:T(8,128)(2,1)S(1)}, u32[]{:S(2)}, u32[]{:S(2)}) collective-permute-start(bf16[18,1,8,192]{3,2,1,0:T(8,128)(2,1)S(1)} %get-tuple-element.10), channel_id=1, source_target_pairs={{0,1},{1,2},{2,3},{3,4},{4,5},{5,6},{6,7},{7,8},{8,9},{9,10},{10,1... | collective-permute-start | bytes 165896 | tf_op jit(solution)/shard_map/ppermute | solution.py:16
  136.9 2.1 %collective-permute-start.7 = (bf16[18,1,8,192]{3,2,1,0:T(8,128)(2,1)S(1)}, bf16[18,1,8,192]{3,2,1,0:T(8,128)(2,1)S(1)}, u32[]{:S(2)}, u32[]{:S(2)}) collective-permute-start(bf16[18,1,8,192]{3,2,1,0:T(8,128)(2,1)S(1)} %get-tuple-element.9), channel_id=1, source_target_pairs={{1,0},{2,1},{3,2},{4,3},{5,4},{6,5},{7,6},{8,7},{9,8},{10,9},{11,1... | collective-permute-start | bytes 165896 | tf_op jit(solution)/shard_map/ppermute | solution.py:19
  139.0 7.5 %collective-permute-done.7 = bf16[18,1,8,192]{3,2,1,0:T(8,128)(2,1)S(1)} collective-permute-done((bf16[18,1,8,192]{3,2,1,0:T(8,128)(2,1)S(1)}, bf16[18,1,8,192]{3,2,1,0:T(8,128)(2,1)S(1)}, u32[]{:S(2)}, u32[]{:S(2)}) %collective-permute-start.7) | collective-permute-done | bytes 55328 | tf_op jit(solution)/shard_map/ppermute | solution.py:19
  146.5 0.3 fusion.3
  146.7 1.2 fusion.15
  148.0 2.5 %pad_slice_fusion = (bf16[8,8,8,192]{3,2,1,0:T(8,128)(2,1)}, bf16[8,8,8,192]{3,2,1,0:T(8,128)(2,1)}, bf16[8,8,8,192]{3,2,1,0:T(8,128)(2,1)}, bf16[8,8,8,192]{3,2...) fusion(bf16[10,10,8,192]{3,2,1,0:T(8,128)(2,1)S(1)} %fusion.3), kind=kLoop, calls=%fused_computation.1 | loop fusion | bytes 4669440 | tf_op jit(solution)/shard_map/slice | solution.py:45
  150.4 10.0 %concatenate.23 = bf16[512,5184]{1,0:T(8,128)(2,1)} concatenate(bf16[512,192]{1,0:T(8,128)(2,1)} %bitcast.122, bf16[512,192]{1,0:T(8,128)(2,1)} %bitcast.121, bf16[512,192]{1,0:T(8,128)(2,1)} %bitcast.132, bf16[512,192]{1,0:T(8,128)(2,1)} %bitcast.133, bf16[512,192]{1,0:T(8,128)(2,1)} %bitcast.120, bf16[512,192]{1,0:T(8,128)(2,1)} %bitcast.134, bf16[512,192]{1,0:T(8,128)(2,1)} %bitcast.135, ...), dimensions={1} | concatenate | bytes 10616832 | tf_op jit(solution)/shard_map/concatenate | solution.py:47
  160.4 0.5 reduce_sum.21
  160.9 6.7 %convert_element_type.78 = bf16[324,32,6]{2,1,0:T(8,128)(2,1)} reshape(bf16[12,5184]{1,0:T(8,128)(2,1)S(1)} %reduce_sum.21) | data formatting | bytes 248832 | tf_op jit(solution)/shard_map/convert_element_type | solution.py:74
  167.6 3.9 %copy.16 = bf16[32,324,6]{0,2,1:T(8,128)(2,1)S(1)} copy(bf16[32,324,6]{2,0,1:T(8,128)(2,1)} %bitcast.93) | data formatting | bytes 248832 | tf_op jit(solution)/shard_map/convert_element_type | solution.py:74
  171.5 1.1 convert_element_type.80
  172.6 0.5 broadcast.18
  173.1 2.1 %reduce.4 = bf16[32,1944]{0,1:T(8,128)(2,1)S(1)} reduce(bf16[32,1,1944]{0,2,1:T(8,128)(2,1)} %convert_element_type.80, bf16[]{:T(256)} %broadcast.18), dimensions={1}, to_apply=%copy.17.reduce_sub_computation | reduce | bytes 248834 | tf_op jit(solution)/shard_map/convert_element_type | solution.py:74
  175.2 0.2 copy.19
  175.4 0.9 reshape.279
  176.3 11.6 %all-to-all-start.1 = ((bf16[32,2,972]{2,1,0:T(2,128)(2,1)}), bf16[32,2,972]{2,1,0:T(2,128)(2,1)S(1)}, u32[]{:S(2)}, u32[]{:S(2)}) async-start(bf16[32,2,972]{2,1,0:T(2,128)(2,1)} %reshape.279), calls=%async_computation.1 | async-start | bytes 262144 | tf_op jit(solution)/shard_map/all_to_all | solution.py:74
  188.0 5.1 %fusion.1 = bf16[1,1,1,192,512]{4,3,2,1,0:T(8,128)(2,1)} fusion(bf16[512,5184]{1,0:T(8,128)(2,1)} %concatenate.23, bf16[5184,192]{1,0:T(8,128)(2,1)S(1)} %bitcast.92, f32[512]{0:T(512)S(1)} %convert_element_type.70), kind=kOutput, calls=%fused_computation.50 | convolution fusion | flops 1019412480 | bytes 7497728 | tf_op jit(solution)/shard_map/ki,vk->iv/dot_general | solution.py:66
  193.1 7.2 %all-to-all-done.1 = bf16[32,2,972]{2,1,0:T(2,128)(2,1)S(1)} async-done(((bf16[32,2,972]{2,1,0:T(2,128)(2,1)}), bf16[32,2,972]{2,1,0:T(2,128)(2,1)S(1)}, u32[]{:S(2)}, u32[]{:S(2)}) %all-to-all-start.1) | async-done | bytes 124448 | tf_op jit(solution)/shard_map/all_to_all | solution.py:74
  200.3 0.2 reshape.280
  200.5 0.2 convert_reduce_fusion
  200.7 0.1 div.27
  200.9 0.8 copy.18
  (21 shorter events, 0.2 us)
Async XLA Ops:
  0.6 21.5 %copy-start.1 = (bf16[192,27,192]{2,0,1:T(8,128)(2,1)S(1)}, bf16[192,27,192]{2,0,1:T(8,128)(2,1)}, u32[]{:S(2)}) copy-start(bf16[192,27,192]{2,0,1:T(8,128)(2,1)} %param.8) | copy-start | bytes 5971972
  3.5 8.6 %copy-start.3 = (bf16[16,16,8,192]{3,2,1,0:T(8,128)(2,1)}, bf16[16,16,8,192]{3,2,1,0:T(8,128)(2,1)S(1)}, u32[]{:S(2)}) copy-start(bf16[16,16,8,192]{3,2,1,0:T(8,128)(2,1)S(1)} %constant_dynamic-update-slice_fusion.1) | copy-start | bytes 2359300
  3.6 5.3 %collective-permute-start = (bf16[1,16,8,192]{3,2,1,0:T(8,128)(2,1)S(1)}, bf16[1,16,8,192]{3,2,1,0:T(8,128)(2,1)S(1)}, u32[]{:S(2)}, u32[]{:S(2)}) collective-permute-start(bf16[1,16,8,192]{3,2,1,0:T(8,128)(2,1)S(1)} %get-tuple-element.15), channel_id=1, source_target_pairs={{0,32},{32,64},{64,96},{96,128},{128,160},{160,192},{192,224},{224... | collective-permute-start | bytes 147464 | tf_op jit(solution)/shard_map/ppermute | solution.py:16
  6.8 5.3 %collective-permute-start.1 = (bf16[1,16,8,192]{3,2,1,0:T(8,128)(2,1)S(1)}, bf16[1,16,8,192]{3,2,1,0:T(8,128)(2,1)S(1)}, u32[]{:S(2)}, u32[]{:S(2)}) collective-permute-start(bf16[1,16,8,192]{3,2,1,0:T(8,128)(2,1)S(1)} %get-tuple-element.16), channel_id=1, source_target_pairs={{32,0},{64,32},{96,64},{128,96},{160,128},{192,160},{224,192},{256... | collective-permute-start | bytes 147464 | tf_op jit(solution)/shard_map/ppermute | solution.py:19
  12.2 13.4 %collective-permute-start.2 = (bf16[18,1,8,192]{3,2,1,0:T(8,128)(2,1)S(1)}, bf16[18,1,8,192]{3,2,1,0:T(8,128)(2,1)S(1)}, u32[]{:S(2)}, u32[]{:S(2)}) collective-permute-start(bf16[18,1,8,192]{3,2,1,0:T(8,128)(2,1)S(1)} %get-tuple-element.12), channel_id=1, source_target_pairs={{0,1},{1,2},{2,3},{3,4},{4,5},{5,6},{6,7},{7,8},{8,9},{9,10},{10,1... | collective-permute-start | bytes 165896 | tf_op jit(solution)/shard_map/ppermute | solution.py:16
  20.2 9.6 %collective-permute-start.3 = (bf16[18,1,8,192]{3,2,1,0:T(8,128)(2,1)S(1)}, bf16[18,1,8,192]{3,2,1,0:T(8,128)(2,1)S(1)}, u32[]{:S(2)}, u32[]{:S(2)}) collective-permute-start(bf16[18,1,8,192]{3,2,1,0:T(8,128)(2,1)S(1)} %get-tuple-element.11), channel_id=1, source_target_pairs={{1,0},{2,1},{3,2},{4,3},{5,4},{6,5},{7,6},{8,7},{9,8},{10,9},{11,1... | collective-permute-start | bytes 165896 | tf_op jit(solution)/shard_map/ppermute | solution.py:19
  34.8 10.1 %copy-start.4 = (bf16[192,27,192]{0,2,1:T(8,128)(2,1)S(1)}, bf16[192,27,192]{0,2,1:T(8,128)(2,1)}, u32[]{:S(2)}) copy-start(bf16[192,27,192]{0,2,1:T(8,128)(2,1)} %copy.14) | copy-start | bytes 5971972
  44.9 5.5 %copy-start = (bf16[512,5184]{1,0:T(8,128)(2,1)S(1)}, bf16[512,5184]{1,0:T(8,128)(2,1)}, u32[]{:S(2)}) copy-start(bf16[512,5184]{1,0:T(8,128)(2,1)} %concatenate.20) | copy-start | bytes 15925252
  53.9 106.5 %all-to-all-start = ((bf16[16,12,5184]{2,1,0:T(8,128)(2,1)}), bf16[16,12,5184]{2,1,0:T(8,128)(2,1)S(1)}, u32[]{:S(2)}, u32[]{:S(2)}) async-start(bf16[16,12,5184]{2,1,0:T(8,128)(2,1)} %reshape.276), calls=%async_computation | async-start | bytes 5373952 | tf_op jit(solution)/shard_map/all_to_all | solution.py:71
  64.5 56.9 %collective-permute-start.4 = (bf16[1,16,8,192]{3,2,1,0:T(8,128)(2,1)S(1)}, bf16[1,16,8,192]{3,2,1,0:T(8,128)(2,1)S(1)}, u32[]{:S(2)}, u32[]{:S(2)}) collective-permute-start(bf16[1,16,8,192]{3,2,1,0:T(8,128)(2,1)S(1)} %get-tuple-element.13), channel_id=1, source_target_pairs={{0,32},{32,64},{64,96},{96,128},{128,160},{160,192},{192,224},{224... | collective-permute-start | bytes 147464 | tf_op jit(solution)/shard_map/ppermute | solution.py:16
  67.6 54.8 %collective-permute-start.5 = (bf16[1,16,8,192]{3,2,1,0:T(8,128)(2,1)S(1)}, bf16[1,16,8,192]{3,2,1,0:T(8,128)(2,1)S(1)}, u32[]{:S(2)}, u32[]{:S(2)}) collective-permute-start(bf16[1,16,8,192]{3,2,1,0:T(8,128)(2,1)S(1)} %get-tuple-element.14), channel_id=1, source_target_pairs={{32,0},{64,32},{96,64},{128,96},{160,128},{192,160},{224,192},{256... | collective-permute-start | bytes 147464 | tf_op jit(solution)/shard_map/ppermute | solution.py:19
  122.4 16.6 %collective-permute-start.6 = (bf16[18,1,8,192]{3,2,1,0:T(8,128)(2,1)S(1)}, bf16[18,1,8,192]{3,2,1,0:T(8,128)(2,1)S(1)}, u32[]{:S(2)}, u32[]{:S(2)}) collective-permute-start(bf16[18,1,8,192]{3,2,1,0:T(8,128)(2,1)S(1)} %get-tuple-element.10), channel_id=1, source_target_pairs={{0,1},{1,2},{2,3},{3,4},{4,5},{5,6},{6,7},{7,8},{8,9},{9,10},{10,1... | collective-permute-start | bytes 165896 | tf_op jit(solution)/shard_map/ppermute | solution.py:16
  136.9 9.6 %collective-permute-start.7 = (bf16[18,1,8,192]{3,2,1,0:T(8,128)(2,1)S(1)}, bf16[18,1,8,192]{3,2,1,0:T(8,128)(2,1)S(1)}, u32[]{:S(2)}, u32[]{:S(2)}) collective-permute-start(bf16[18,1,8,192]{3,2,1,0:T(8,128)(2,1)S(1)} %get-tuple-element.9), channel_id=1, source_target_pairs={{1,0},{2,1},{3,2},{4,3},{5,4},{6,5},{7,6},{8,7},{9,8},{10,9},{11,1... | collective-permute-start | bytes 165896 | tf_op jit(solution)/shard_map/ppermute | solution.py:19
  167.6 20.3 %copy-start.2 = (bf16[192,27,192]{2,0,1:T(8,128)(2,1)S(1)}, bf16[192,27,192]{2,0,1:T(8,128)(2,1)}, u32[]{:S(2)}) copy-start(bf16[192,27,192]{2,0,1:T(8,128)(2,1)} %param.8) | copy-start | bytes 5971972
  176.3 24.0 %all-to-all-start.1 = ((bf16[32,2,972]{2,1,0:T(2,128)(2,1)}), bf16[32,2,972]{2,1,0:T(2,128)(2,1)S(1)}, u32[]{:S(2)}, u32[]{:S(2)}) async-start(bf16[32,2,972]{2,1,0:T(2,128)(2,1)} %reshape.279), calls=%async_computation.1 | async-start | bytes 262144 | tf_op jit(solution)/shard_map/all_to_all | solution.py:74

commit v2 on v1

--- a/solution.py
+++ b/solution.py
@@ -1,8 +1,12 @@
 import jax
 import jax.numpy as jnp
 from jax import lax
+from jax.experimental import pallas as pl
+from jax.experimental.pallas import tpu as pltpu
 from jax.sharding import PartitionSpec as P
 
+MESH = pl.DeviceIdType.MESH
+HALF = 14
 BE = 8
 TX = 2
 TY = 2
@@ -47,6 +51,130 @@
     return jnp.concatenate(pieces, axis=1)
 
 
+def scatter_kernel(
+    part, out, core_rx, mid, x_rx, acc, yb, y_rx, flat, rows, turned, zb, z_rx,
+    core_send, core_recv, x_send, x_recv, y_send, y_recv, z_send, z_recv, fin_send, fin_recv,
+):
+    gx, gy = lax.axis_index("gx"), lax.axis_index("gy")
+    x, y = lax.div(gx, 4), lax.rem(gx, 4)
+    q, core = lax.div(gy, 2), lax.rem(gy, 2)
+    other = 1 - core
+    partner = (gx, 2 * q + other)
+    x_of = [lax.rem(x + k, 4) for k in range(4)]
+    y_of = [lax.rem(y + k, 4) for k in range(4)]
+    q_of = [lax.rem(q + k, 16) for k in range(16)]
+    x_peer = [(4 * x_of[k] + y, gy) for k in range(4)]
+    y_peer = [(4 * x + y_of[k], gy) for k in range(4)]
+    q_peer = [(gx, 2 * q_of[k] + core) for k in range(16)]
+
+    barrier = pltpu.get_barrier_semaphore()
+    peers = [partner] + x_peer[1:] + y_peer[1:] + q_peer[1:]
+    for peer in peers:
+        pl.semaphore_signal(barrier, inc=1, device_id=peer, device_id_type=MESH)
+    pl.semaphore_wait(barrier, len(peers))
+
+    def remote(src, dst, send, recv, peer):
+        return pltpu.make_async_remote_copy(
+            src_ref=src, dst_ref=dst, send_sem=send, recv_sem=recv,
+            device_id=peer, device_id_type=MESH,
+        )
+
+    order = (2, 1, 3, 0)
+    core_copy = {
+        k: remote(
+            part.at[other, x_of[k]], core_rx.at[x_of[k]], core_send.at[k], core_recv.at[k], partner
+        )
+        for k in order
+    }
+    for k in order:
+        core_copy[k].start()
+    x_copy = {
+        k: remote(mid.at[x_of[k]], x_rx.at[k - 1], x_send.at[k - 1], x_recv.at[k - 1], x_peer[k])
+        for k in (2, 1, 3)
+    }
+    acc[48:56, :] = jnp.zeros((8, acc.shape[1]), jnp.float32)
+    rows[...] = jnp.zeros(rows.shape, jnp.float32)
+    for k in order:
+        core_copy[k].wait_recv()
+        total = part[core, x_of[k]].astype(jnp.float32) + core_rx[x_of[k]].astype(jnp.float32)
+        if k:
+            mid[x_of[k]] = total.astype(jnp.bfloat16)
+            x_copy[k].start()
+        else:
+            acc[0:48, :] = total
+    for k in (1, 3, 2):
+        x_copy[k].wait_recv()
+        acc[0:48, :] += x_rx[k - 1].astype(jnp.float32)
+    for j in range(4):
+        yb[j] = acc[12 * j : 12 * j + 16, :].astype(jnp.bfloat16)
+    y_copy = {
+        k: remote(yb.at[y_of[k]], y_rx.at[k - 1], y_send.at[k - 1], y_recv.at[k - 1], y_peer[k])
+        for k in (2, 1, 3)
+    }
+    for k in (2, 1, 3):
+        y_copy[k].start()
+    total = yb[y].astype(jnp.float32)
+    for k in (1, 3, 2):
+        y_copy[k].wait_recv()
+        total = total + y_rx[k - 1].astype(jnp.float32)
+    flat[...] = total
+    width = flat.shape[1] // HALF
+    for t in range(HALF):
+        rows[16 * t : 16 * t + 16, 0:width] = flat[:, width * t : width * t + width]
+    turned[...] = rows[...].T
+    for j in range(16):
+        zb[j] = turned[12 * j : 12 * j + 16, :].astype(jnp.bfloat16)
+    z_copy = [
+        remote(zb.at[q_of[k]], z_rx.at[k - 1], z_send.at[k - 1], z_recv.at[k - 1], q_peer[k])
+        for k in range(1, 16)
+    ]
+    for copy in z_copy:
+        copy.start()
+    total = zb[q].astype(jnp.float32)
+    for k, copy in enumerate(z_copy):
+        copy.wait_recv()
+        total = total + z_rx[k].astype(jnp.float32)
+    out[core] = total
+    last = remote(out.at[core], out.at[core], fin_send, fin_recv, partner)
+    last.start()
+    for k in order:
+        core_copy[k].wait_send()
+    for k in (2, 1, 3):
+        x_copy[k].wait_send()
+        y_copy[k].wait_send()
+    for copy in z_copy:
+        copy.wait_send()
+    last.wait()
+
+
+def scattered(part):
+    depth = part.shape[3]
+    bf, f32 = jnp.bfloat16, jnp.float32
+    dma = pltpu.SemaphoreType.DMA
+    return pl.pallas_call(
+        scatter_kernel,
+        out_shape=jax.ShapeDtypeStruct((2, 16, 256), f32),
+        in_specs=[pl.BlockSpec(memory_space=pltpu.VMEM)],
+        out_specs=pl.BlockSpec(memory_space=pltpu.VMEM),
+        scratch_shapes=[
+            pltpu.VMEM((4, 48, depth), bf),
+            pltpu.VMEM((4, 48, depth), bf),
+            pltpu.VMEM((3, 48, depth), bf),
+            pltpu.VMEM((56, depth), f32),
+            pltpu.VMEM((4, 16, depth), bf),
+            pltpu.VMEM((3, 16, depth), bf),
+            pltpu.VMEM((16, depth), f32),
+            pltpu.VMEM((256, 256), f32),
+            pltpu.VMEM((256, 256), f32),
+            pltpu.VMEM((16, 16, 256), bf),
+            pltpu.VMEM((15, 16, 256), bf),
+            dma((4,)), dma((4,)), dma((3,)), dma((3,)), dma((3,)), dma((3,)),
+            dma((15,)), dma((15,)), dma, dma,
+        ],
+        compiler_params=pltpu.CompilerParams(collective_id=0, has_side_effects=True),
+    )(part)
+
+
 def shards(features, occupancy, brick_pos, weight, cotangent):
     x = features[0, 0, 0]
     channels, voxels = x.shape
@@ -60,20 +188,20 @@
     maskf = mask.astype(jnp.float32)
     output = (jax.nn.silu(pre) * maskf).astype(jnp.bfloat16)
     g = (cotangent[0, 0, 0].astype(jnp.float32) * silu_slope(pre) * maskf).astype(jnp.bfloat16)
-    wsum = jnp.einsum("ov,vk->ok", g, cols, preferred_element_type=jnp.float32)
     gcols = columns_of(g.T, start, True)
+    cut = HALF * channels
+    low = jnp.einsum("ov,vk->ok", g, cols[:, :cut], preferred_element_type=jnp.float32)
+    high = jnp.einsum("ov,vk->ok", g, cols[:, cut:], preferred_element_type=jnp.float32)
+    high = jnp.pad(high, ((0, 0), (0, 2 * cut - 27 * channels)))
+    part = jnp.stack([low, high]).astype(jnp.bfloat16).reshape(2, 4, 48, cut)
+    part, gcols = lax.optimization_barrier((part, gcols))
     w_bwd = weight.transpose(1, 0, 2).reshape(27 * channels, channels)
     back = jnp.einsum("ki,vk->iv", w_bwd, gcols, preferred_element_type=jnp.float32)
     x_grad = (back * maskf).astype(jnp.bfloat16)
-    nx, ny = lax.axis_size("gx"), lax.axis_size("gy")
-    rows, colw = channels // nx, channels // ny
-    part = wsum.astype(jnp.bfloat16).reshape(nx, rows, 27 * channels)
-    part = lax.all_to_all(part, "gx", 0, 0)
-    part = part.astype(jnp.float32).sum(0)
-    part = part.reshape(rows * 27, ny, colw).transpose(1, 0, 2).reshape(ny, rows * 27 * colw)
-    part = lax.all_to_all(part.astype(jnp.bfloat16), "gy", 0, 0)
-    part = part.astype(jnp.float32).sum(0)
-    w_grad = part.reshape(rows, 27, colw) / (nx * ny)
+    total = scattered(part)
+    mine = lax.dynamic_slice(total, (0, lax.axis_index("gy") % 2 * 6, 0), (2, 6, 16 * HALF))
+    mine = mine.reshape(2, 6, HALF, 16)[:, :, :, :12].transpose(3, 0, 2, 1)
+    w_grad = mine.reshape(12, 2 * HALF, 6)[:, :27] / (lax.axis_size("gx") * lax.axis_size("gy"))
     return (output[None, None, None], x_grad[None, None, None], w_grad)
 
 

time: 204 us -> 163 us (0.80)
  the two profiles are of different devices: /device:TPU:11 before, /device:TPU:57 now
where the time goes in v2:
time: 163 us; the launch traced here: 160 us
  Pallas kernels  50 us (31%)
  local copies, waits for them, and re-layouts  42.8 us (26%)
  starting transfers between devices  31.4 us (19%)
  matrix products  15.4 us (9%)
  waiting for transfers between devices  14.2 us (9%)
  other arithmetic  4.56 us (3%)
  between operations  1.92 us (1%)
    pallas_call x1, Pallas kernels, scattered(): pl.pallas_call(scatter_kernel, out_shape=jax.ShapeDtypeStruct((2, 16, 256...  50 us
    concatenate x4, local copies, waits for them, and re-layouts, columns_of(): return jnp.concatenate(pieces, axis=1)  31.6 us
    ppermute x4, starting transfers between devices, extended(): lax.ppermute(lax.slice_in_dim(block, block.shape[dim] - width, None, axis...  22.7 us
    ppermute x4, waiting for transfers between devices, extended(): lax.ppermute(lax.slice_in_dim(block, 0, width, axis=dim), axis, backward)  12.9 us
    ppermute x4, starting transfers between devices, extended(): lax.ppermute(lax.slice_in_dim(block, 0, width, axis=dim), axis, backward)  8.74 us
    dot_general x1, matrix products, shards(): jnp.einsum('ok,vk->ov', w_fwd, cols, preferred_element_type=jnp.float32)  6.1 us
    dot_general x1, matrix products, shards(): jnp.einsum('ki,vk->iv', w_bwd, gcols, preferred_element_type=jnp.float32)  5.12 us
    slice x4, local copies, waits for them, and re-layouts, columns_of(): view = window[s[0]:s[0] + BE, s[1]:s[1] + BE, s[2]:s[2] + BE, :]  5.01 us
  transfers between devices with their start and end apart: 8, of which 3 were waited for; matrix products, arithmetic and copies ran while one was open for 5% of the time, Pallas kernels for 0%

profile of v2, /device:TPU:57, one launch (start us, length us, event | category | flops | bytes accessed | tf_op | source)
XLA Modules:
  0.0 160.3 jit_solution(4619640578627935564)
XLA Ops:
  0.6 0.0 copy-start
  1.5 0.7 convert_reduce_fusion
  2.2 1.1 copy.13
  3.2 0.1 bitcast_multiply_fusion
  3.4 0.1 broadcast.17.clone
  3.6 3.0 %collective-permute-start.1 = (bf16[1,16,8,192]{3,2,1,0:T(8,128)(2,1)S(1)}, bf16[1,16,8,192]{3,2,1,0:T(8,128)(2,1)S(1)}, u32[]{:S(2)}, u32[]{:S(2)}) collective-permute-start(bf16[1,16,8,192]{3,2,1,0:T(8,128)(2,1)S(1)} %get-tuple-element.14), channel_id=1, source_target_pairs={{32,0},{64,32},{96,64},{128,96},{160,128},{192,160},{224,192},{256... | collective-permute-start | bytes 147464 | tf_op jit(solution)/shard_map/ppermute | solution.py:23
  6.5 5.0 %collective-permute-start = (bf16[1,16,8,192]{3,2,1,0:T(8,128)(2,1)S(1)}, bf16[1,16,8,192]{3,2,1,0:T(8,128)(2,1)S(1)}, u32[]{:S(2)}, u32[]{:S(2)}) collective-permute-start(bf16[1,16,8,192]{3,2,1,0:T(8,128)(2,1)S(1)} %get-tuple-element.13), channel_id=1, source_target_pairs={{0,32},{32,64},{64,96},{96,128},{128,160},{160,192},{192,224},{224... | collective-permute-start | bytes 147464 | tf_op jit(solution)/shard_map/ppermute | solution.py:20
  11.5 0.0 collective-permute-done.1
  11.6 1.3 collective-permute-done
  12.9 7.9 %collective-permute-start.2 = (bf16[18,1,8,192]{3,2,1,0:T(8,128)(2,1)S(1)}, bf16[18,1,8,192]{3,2,1,0:T(8,128)(2,1)S(1)}, u32[]{:S(2)}, u32[]{:S(2)}) collective-permute-start(bf16[18,1,8,192]{3,2,1,0:T(8,128)(2,1)S(1)} %get-tuple-element.10), channel_id=1, source_target_pairs={{0,1},{1,2},{2,3},{3,4},{4,5},{5,6},{6,7},{7,8},{8,9},{9,10},{10,1... | collective-permute-start | bytes 165896 | tf_op jit(solution)/shard_map/ppermute | solution.py:20
  20.8 1.9 %collective-permute-start.3 = (bf16[18,1,8,192]{3,2,1,0:T(8,128)(2,1)S(1)}, bf16[18,1,8,192]{3,2,1,0:T(8,128)(2,1)S(1)}, u32[]{:S(2)}, u32[]{:S(2)}) collective-permute-start(bf16[18,1,8,192]{3,2,1,0:T(8,128)(2,1)S(1)} %get-tuple-element.9), channel_id=1, source_target_pairs={{1,0},{2,1},{3,2},{4,3},{5,4},{6,5},{7,6},{8,7},{9,8},{10,9},{11,1... | collective-permute-start | bytes 165896 | tf_op jit(solution)/shard_map/ppermute | solution.py:23
  22.8 0.0 copy-done
  22.8 3.4 %copy.14 = bf16[192,27,192]{0,2,1:T(8,128)(2,1)} copy(bf16[192,27,192]{2,0,1:T(8,128)(2,1)S(1)} %copy-done) | data formatting | bytes 3981312 | tf_op args[3]
  26.3 0.0 collective-permute-done.2
  26.3 5.8 %collective-permute-done.3 = bf16[18,1,8,192]{3,2,1,0:T(8,128)(2,1)S(1)} collective-permute-done((bf16[18,1,8,192]{3,2,1,0:T(8,128)(2,1)S(1)}, bf16[18,1,8,192]{3,2,1,0:T(8,128)(2,1)S(1)}, u32[]{:S(2)}, u32[]{:S(2)}) %collective-permute-start.3) | collective-permute-done | bytes 55328 | tf_op jit(solution)/shard_map/ppermute | solution.py:23
  32.1 1.2 fusion.7
  33.4 0.2 fusion.16
  33.6 2.3 %pad_slice_fusion.18 = (bf16[8,8,8,192]{3,2,1,0:T(8,128)(2,1)}, bf16[8,8,8,192]{3,2,1,0:T(8,128)(2,1)S(1)}, bf16[8,8,8,192]{3,2,1,0:T(8,128)(2,1)S(1)}, bf16[8,8...) fusion(bf16[10,10,8,192]{3,2,1,0:T(8,128)(2,1)S(1)} %fusion.7), kind=kLoop, calls=%fused_computation.20 | loop fusion | bytes 4669440 | tf_op jit(solution)/shard_map/slice | solution.py:49
  35.9 5.9 %concatenate.32 = bf16[512,2496]{1,0:T(8,128)(2,1)} concatenate(bf16[512,192]{1,0:T(8,128)(2,1)} %bitcast.137, bf16[512,192]{1,0:T(8,128)(2,1)} %bitcast.139, bf16[512,192]{1,0:T(8,128)(2,1)S(1)} %bitcast.117, bf16[512,192]{1,0:T(8,128)(2,1)} %bitcast.141, bf16[512,192]{1,0:T(8,128)(2,1)} %bitcast.143, bf16[512,192]{1,0:T(8,128)(2,1)} %bitcast.155, bf16[512,192]{1,0:T(8,128)(2,1)} %bitcast.145, ...), dimensions={1} | concatenate | bytes 5111808 | tf_op jit(solution)/shard_map/concatenate | solution.py:51
  41.9 10.5 %concatenate.30 = bf16[512,5184]{1,0:T(8,128)(2,1)} concatenate(bf16[512,192]{1,0:T(8,128)(2,1)S(1)} %bitcast.113, bf16[512,192]{1,0:T(8,128)(2,1)S(1)} %bitcast.111, bf16[512,192]{1,0:T(8,128)(2,1)S(1)} %bitcast.119, bf16[512,192]{1,0:T(8,128)(2,1)S(1)} %bitcast.121, bf16[512,192]{1,0:T(8,128)(2,1)S(1)} %bitcast.109, bf16[512,192]{1,0:T(8,128)(2,1)S(1)} %bitcast.123, ...), dimensions={1} | concatenate | bytes 10616832 | tf_op jit(solution)/shard_map/concatenate | solution.py:51
  52.4 5.0 %concatenate.31 = bf16[512,2688]{1,0:T(8,128)(2,1)S(1)} concatenate(bf16[512,192]{1,0:T(8,128)(2,1)} %bitcast.114, bf16[512,192]{1,0:T(8,128)(2,1)} %bitcast.112, bf16[512,192]{1,0:T(8,128)(2,1)} %bitcast.120, bf16[512,192]{1,0:T(8,128)(2,1)} %bitcast.122, bf16[512,192]{1,0:T(8,128)(2,1)} %bitcast.110, bf16[512,192]{1,0:T(8,128)(2,1)} %bitcast.124, bf16[512,192]{1,0:T(8,128)(2,1)} %bitcast.126, ...), dimensions={1} | concatenate | bytes 5505024 | tf_op jit(solution)/shard_map/concatenate | solution.py:51
  57.4 6.1 %fusion.11 = (bf16[192,512]{1,0:T(8,128)(2,1)S(1)}, bf16[1,1,1,192,512]{4,3,2,1,0:T(8,128)(2,1)}) fusion(bf16[1,1,1,192,512]{4,3,2,1,0:T(8,128)(2,1)} %param.9, f32[512]{0:T(512)S(1)} %convert_element_type.49, bf16[512,5184]{1,0:T(8,128)(2,1)} %concatenate.30, bf16[192,5184]{0,1:T(8,128)(2,1)} %bitcast.102), kind=kOutput, calls=%fused_computation.63 | convolution fusion | flops 1020592128 | bytes 7890944 | tf_op jit(solution)/shard_map/ok,vk->ov/dot_general | solution.py:187
  63.5 1.7 %convolution_convert_fusion.1 = bf16[192,2688]{1,0:T(8,128)(2,1)} fusion(bf16[192,512]{1,0:T(8,128)(2,1)S(1)} %get-tuple-element.69, bf16[512,2688]{1,0:T(8,128)(2,1)S(1)} %concatenate.31), kind=kOutput, calls=%fused_computation.1 | convolution fusion | flops 528998400 | bytes 3981312 | tf_op jit(solution)/shard_map/ov,vk->ok/dot_general | solution.py:193
  65.2 0.1 copy.15
  65.4 0.1 broadcast.17
  65.5 1.9 %collective-permute-start.5 = (bf16[1,16,8,192]{3,2,1,0:T(8,128)(2,1)S(1)}, bf16[1,16,8,192]{3,2,1,0:T(8,128)(2,1)S(1)}, u32[]{:S(2)}, u32[]{:S(2)}) collective-permute-start(bf16[1,16,8,192]{3,2,1,0:T(8,128)(2,1)S(1)} %get-tuple-element.12), channel_id=1, source_target_pairs={{32,0},{64,32},{96,64},{128,96},{160,128},{192,160},{224,192},{256... | collective-permute-start | bytes 147464 | tf_op jit(solution)/shard_map/ppermute | solution.py:23
  67.4 6.2 %collective-permute-start.4 = (bf16[1,16,8,192]{3,2,1,0:T(8,128)(2,1)S(1)}, bf16[1,16,8,192]{3,2,1,0:T(8,128)(2,1)S(1)}, u32[]{:S(2)}, u32[]{:S(2)}) collective-permute-start(bf16[1,16,8,192]{3,2,1,0:T(8,128)(2,1)S(1)} %get-tuple-element.11), channel_id=1, source_target_pairs={{0,32},{32,64},{64,96},{96,128},{128,160},{160,192},{192,224},{224... | collective-permute-start | bytes 147464 | tf_op jit(solution)/shard_map/ppermute | solution.py:20
  73.6 2.4 %convolution_convert_fusion = bf16[192,2496]{1,0:T(8,128)(2,1)S(1)} fusion(bf16[192,512]{1,0:T(8,128)(2,1)S(1)} %get-tuple-element.69, bf16[512,2496]{1,0:T(8,128)(2,1)} %concatenate.32), kind=kOutput, calls=%fused_computation | convolution fusion | flops 491212800 | bytes 3710976 | tf_op jit(solution)/shard_map/ov,vk->ok/dot_general | solution.py:194
  76.1 0.1 pad.13
  76.2 0.0 collective-permute-done.5
  76.2 0.0 collective-permute-done.4
  76.2 3.5 %collective-permute-start.6 = (bf16[18,1,8,192]{3,2,1,0:T(8,128)(2,1)S(1)}, bf16[18,1,8,192]{3,2,1,0:T(8,128)(2,1)S(1)}, u32[]{:S(2)}, u32[]{:S(2)}) collective-permute-start(bf16[18,1,8,192]{3,2,1,0:T(8,128)(2,1)S(1)} %get-tuple-element.8), channel_id=1, source_target_pairs={{0,1},{1,2},{2,3},{3,4},{4,5},{5,6},{6,7},{7,8},{8,9},{9,10},{10,1... | collective-permute-start | bytes 165896 | tf_op jit(solution)/shard_map/ppermute | solution.py:20
  79.8 1.9 %collective-permute-start.7 = (bf16[18,1,8,192]{3,2,1,0:T(8,128)(2,1)S(1)}, bf16[18,1,8,192]{3,2,1,0:T(8,128)(2,1)S(1)}, u32[]{:S(2)}, u32[]{:S(2)}) collective-permute-start(bf16[18,1,8,192]{3,2,1,0:T(8,128)(2,1)S(1)} %get-tuple-element.7), channel_id=1, source_target_pairs={{1,0},{2,1},{3,2},{4,3},{5,4},{6,5},{7,6},{8,7},{9,8},{10,9},{11,1... | collective-permute-start | bytes 165896 | tf_op jit(solution)/shard_map/ppermute | solution.py:23
  81.7 1.5 pad_maximum_fusion.part
  83.2 0.0 collective-permute-done.6
  83.2 7.0 %collective-permute-done.7 = bf16[18,1,8,192]{3,2,1,0:T(8,128)(2,1)S(1)} collective-permute-done((bf16[18,1,8,192]{3,2,1,0:T(8,128)(2,1)S(1)}, bf16[18,1,8,192]{3,2,1,0:T(8,128)(2,1)S(1)}, u32[]{:S(2)}, u32[]{:S(2)}) %collective-permute-start.7) | collective-permute-done | bytes 55328 | tf_op jit(solution)/shard_map/ppermute | solution.py:23
  90.2 0.3 fusion.3
  90.5 0.2 fusion.15
  90.7 2.4 %pad_slice_fusion = (bf16[8,8,8,192]{3,2,1,0:T(8,128)(2,1)S(1)}, bf16[8,8,8,192]{3,2,1,0:T(8,128)(2,1)S(1)}, bf16[8,8,8,192]{3,2,1,0:T(8,128)(2,1)S(1)}, bf16[8,...) fusion(bf16[10,10,8,192]{3,2,1,0:T(8,128)(2,1)S(1)} %fusion.3), kind=kLoop, calls=%fused_computation.2 | loop fusion | bytes 4669440 | tf_op jit(solution)/shard_map/slice | solution.py:49
  93.0 10.3 %concatenate.35 = bf16[512,5184]{1,0:T(8,128)(2,1)} concatenate(bf16[512,192]{1,0:T(8,128)(2,1)S(1)} %bitcast.165, bf16[512,192]{1,0:T(8,128)(2,1)S(1)} %bitcast.164, bf16[512,192]{1,0:T(8,128)(2,1)S(1)} %bitcast.167, bf16[512,192]{1,0:T(8,128)(2,1)S(1)} %bitcast.168, bf16[512,192]{1,0:T(8,128)(2,1)S(1)} %bitcast.163, bf16[512,192]{1,0:T(8,128)(2,1)S(1)} %bitcast.169, ...), dimensions={1} | concatenate | bytes 10616832 | tf_op jit(solution)/shard_map/concatenate | solution.py:51
  103.3 0.0 copy-start.1
  103.3 50.0 %shard_map.76 = f32[2,16,256]{2,1,0:T(8,128)} custom-call(bf16[2,4,48,2688]{3,2,1,0:T(8,128)(2,1)} %pad_maximum_fusion.part), custom_call_target="tpu_custom_call" | custom-call | tf_op jit(solution)/shard_map/pallas_call | solution.py:154
  153.3 0.8 constant_dynamic-slice_fusion
  154.1 0.1 reshape.266
  154.2 0.2 copy.17
  154.4 0.1 reshape.267
  154.5 0.6 slice_multiply_fusion
  155.1 5.1 %fusion.1 = bf16[1,1,1,192,512]{4,3,2,1,0:T(8,128)(2,1)} fusion(bf16[512,5184]{1,0:T(8,128)(2,1)} %concatenate.35, bf16[5184,192]{1,0:T(8,128)(2,1)S(1)} %bitcast.99, f32[512]{0:T(512)S(1)} %convert_element_type.49), kind=kOutput, calls=%fused_computation.52 | convolution fusion | flops 1019412480 | bytes 7497728 | tf_op jit(solution)/shard_map/ki,vk->iv/dot_general | solution.py:199
  (30 shorter events, 0.2 us)
Async XLA Ops:
  0.6 22.2 %copy-start = (bf16[192,27,192]{2,0,1:T(8,128)(2,1)S(1)}, bf16[192,27,192]{2,0,1:T(8,128)(2,1)}, u32[]{:S(2)}) copy-start(bf16[192,27,192]{2,0,1:T(8,128)(2,1)} %param.8) | copy-start | bytes 5971972
  3.5 9.3 %copy-start.2 = (bf16[16,16,8,192]{3,2,1,0:T(8,128)(2,1)}, bf16[16,16,8,192]{3,2,1,0:T(8,128)(2,1)S(1)}, u32[]{:S(2)}) copy-start(bf16[16,16,8,192]{3,2,1,0:T(8,128)(2,1)S(1)} %constant_dynamic-update-slice_fusion.1) | copy-start | bytes 2359300
  3.6 8.0 %collective-permute-start.1 = (bf16[1,16,8,192]{3,2,1,0:T(8,128)(2,1)S(1)}, bf16[1,16,8,192]{3,2,1,0:T(8,128)(2,1)S(1)}, u32[]{:S(2)}, u32[]{:S(2)}) collective-permute-start(bf16[1,16,8,192]{3,2,1,0:T(8,128)(2,1)S(1)} %get-tuple-element.14), channel_id=1, source_target_pairs={{32,0},{64,32},{96,64},{128,96},{160,128},{192,160},{224,192},{256... | collective-permute-start | bytes 147464 | tf_op jit(solution)/shard_map/ppermute | solution.py:23
  6.5 6.3 %collective-permute-start = (bf16[1,16,8,192]{3,2,1,0:T(8,128)(2,1)S(1)}, bf16[1,16,8,192]{3,2,1,0:T(8,128)(2,1)S(1)}, u32[]{:S(2)}, u32[]{:S(2)}) collective-permute-start(bf16[1,16,8,192]{3,2,1,0:T(8,128)(2,1)S(1)} %get-tuple-element.13), channel_id=1, source_target_pairs={{0,32},{32,64},{64,96},{96,128},{128,160},{160,192},{192,224},{224... | collective-permute-start | bytes 147464 | tf_op jit(solution)/shard_map/ppermute | solution.py:20
  12.9 13.4 %collective-permute-start.2 = (bf16[18,1,8,192]{3,2,1,0:T(8,128)(2,1)S(1)}, bf16[18,1,8,192]{3,2,1,0:T(8,128)(2,1)S(1)}, u32[]{:S(2)}, u32[]{:S(2)}) collective-permute-start(bf16[18,1,8,192]{3,2,1,0:T(8,128)(2,1)S(1)} %get-tuple-element.10), channel_id=1, source_target_pairs={{0,1},{1,2},{2,3},{3,4},{4,5},{5,6},{6,7},{7,8},{8,9},{9,10},{10,1... | collective-permute-start | bytes 165896 | tf_op jit(solution)/shard_map/ppermute | solution.py:20
  20.8 11.3 %collective-permute-start.3 = (bf16[18,1,8,192]{3,2,1,0:T(8,128)(2,1)S(1)}, bf16[18,1,8,192]{3,2,1,0:T(8,128)(2,1)S(1)}, u32[]{:S(2)}, u32[]{:S(2)}) collective-permute-start(bf16[18,1,8,192]{3,2,1,0:T(8,128)(2,1)S(1)} %get-tuple-element.9), channel_id=1, source_target_pairs={{1,0},{2,1},{3,2},{4,3},{5,4},{6,5},{7,6},{8,7},{9,8},{10,9},{11,1... | collective-permute-start | bytes 165896 | tf_op jit(solution)/shard_map/ppermute | solution.py:23
  33.6 8.3 %copy-start.4 = (bf16[8,8,8,192]{3,2,1,0:T(8,128)(2,1)}, bf16[8,8,8,192]{3,2,1,0:T(8,128)(2,1)S(1)}, u32[]{:S(2)}) copy-start(bf16[8,8,8,192]{3,2,1,0:T(8,128)(2,1)S(1)} %get-tuple-element.66) | copy-start | bytes 589828
  33.6 8.3 %copy-start.5 = (bf16[8,8,8,192]{3,2,1,0:T(8,128)(2,1)}, bf16[8,8,8,192]{3,2,1,0:T(8,128)(2,1)S(1)}, u32[]{:S(2)}) copy-start(bf16[8,8,8,192]{3,2,1,0:T(8,128)(2,1)S(1)} %get-tuple-element.67) | copy-start | bytes 589828
  33.6 8.3 %copy-start.6 = (bf16[8,8,8,192]{3,2,1,0:T(8,128)(2,1)}, bf16[8,8,8,192]{3,2,1,0:T(8,128)(2,1)S(1)}, u32[]{:S(2)}) copy-start(bf16[8,8,8,192]{3,2,1,0:T(8,128)(2,1)S(1)} %get-tuple-element.68) | copy-start | bytes 589828
  35.9 6.0 %copy-start.7 = (bf16[8,8,8,192]{3,2,1,0:T(8,128)(2,1)}, bf16[8,8,8,192]{3,2,1,0:T(8,128)(2,1)S(1)}, u32[]{:S(2)}) copy-start(bf16[8,8,8,192]{3,2,1,0:T(8,128)(2,1)S(1)} %get-tuple-element.43) | copy-start | bytes 589828
  35.9 6.0 %copy-start.8 = (bf16[8,8,8,192]{3,2,1,0:T(8,128)(2,1)}, bf16[8,8,8,192]{3,2,1,0:T(8,128)(2,1)S(1)}, u32[]{:S(2)}) copy-start(bf16[8,8,8,192]{3,2,1,0:T(8,128)(2,1)S(1)} %get-tuple-element.44) | copy-start | bytes 589828
  35.9 6.0 %copy-start.9 = (bf16[8,8,8,192]{3,2,1,0:T(8,128)(2,1)}, bf16[8,8,8,192]{3,2,1,0:T(8,128)(2,1)S(1)}, u32[]{:S(2)}) copy-start(bf16[8,8,8,192]{3,2,1,0:T(8,128)(2,1)S(1)} %get-tuple-element.45) | copy-start | bytes 589828
  35.9 6.0 %copy-start.10 = (bf16[8,8,8,192]{3,2,1,0:T(8,128)(2,1)}, bf16[8,8,8,192]{3,2,1,0:T(8,128)(2,1)S(1)}, u32[]{:S(2)}) copy-start(bf16[8,8,8,192]{3,2,1,0:T(8,128)(2,1)S(1)} %get-tuple-element.46) | copy-start | bytes 589828
  35.9 6.0 %copy-start.11 = (bf16[8,8,8,192]{3,2,1,0:T(8,128)(2,1)}, bf16[8,8,8,192]{3,2,1,0:T(8,128)(2,1)S(1)}, u32[]{:S(2)}) copy-start(bf16[8,8,8,192]{3,2,1,0:T(8,128)(2,1)S(1)} %get-tuple-element.47) | copy-start | bytes 589828
  65.5 10.6 %collective-permute-start.5 = (bf16[1,16,8,192]{3,2,1,0:T(8,128)(2,1)S(1)}, bf16[1,16,8,192]{3,2,1,0:T(8,128)(2,1)S(1)}, u32[]{:S(2)}, u32[]{:S(2)}) collective-permute-start(bf16[1,16,8,192]{3,2,1,0:T(8,128)(2,1)S(1)} %get-tuple-element.12), channel_id=1, source_target_pairs={{32,0},{64,32},{96,64},{128,96},{160,128},{192,160},{224,192},{256... | collective-permute-start | bytes 147464 | tf_op jit(solution)/shard_map/ppermute | solution.py:23
  67.4 14.2 %copy-start.3 = (bf16[192,2688]{1,0:T(8,128)(2,1)S(1)}, bf16[192,2688]{1,0:T(8,128)(2,1)}, u32[]{:S(2)}) copy-start(bf16[192,2688]{1,0:T(8,128)(2,1)} %convolution_convert_fusion.1) | copy-start | bytes 3096580
  67.4 8.7 %collective-permute-start.4 = (bf16[1,16,8,192]{3,2,1,0:T(8,128)(2,1)S(1)}, bf16[1,16,8,192]{3,2,1,0:T(8,128)(2,1)S(1)}, u32[]{:S(2)}, u32[]{:S(2)}) collective-permute-start(bf16[1,16,8,192]{3,2,1,0:T(8,128)(2,1)S(1)} %get-tuple-element.11), channel_id=1, source_target_pairs={{0,32},{32,64},{64,96},{96,128},{128,160},{160,192},{192,224},{224... | collective-permute-start | bytes 147464 | tf_op jit(solution)/shard_map/ppermute | solution.py:20
  76.2 7.0 %collective-permute-start.6 = (bf16[18,1,8,192]{3,2,1,0:T(8,128)(2,1)S(1)}, bf16[18,1,8,192]{3,2,1,0:T(8,128)(2,1)S(1)}, u32[]{:S(2)}, u32[]{:S(2)}) collective-permute-start(bf16[18,1,8,192]{3,2,1,0:T(8,128)(2,1)S(1)} %get-tuple-element.8), channel_id=1, source_target_pairs={{0,1},{1,2},{2,3},{3,4},{4,5},{5,6},{6,7},{7,8},{8,9},{9,10},{10,1... | collective-permute-start | bytes 165896 | tf_op jit(solution)/shard_map/ppermute | solution.py:20
  79.8 10.5 %collective-permute-start.7 = (bf16[18,1,8,192]{3,2,1,0:T(8,128)(2,1)S(1)}, bf16[18,1,8,192]{3,2,1,0:T(8,128)(2,1)S(1)}, u32[]{:S(2)}, u32[]{:S(2)}) collective-permute-start(bf16[18,1,8,192]{3,2,1,0:T(8,128)(2,1)S(1)} %get-tuple-element.7), channel_id=1, source_target_pairs={{1,0},{2,1},{3,2},{4,3},{5,4},{6,5},{7,6},{8,7},{9,8},{10,9},{11,1... | collective-permute-start | bytes 165896 | tf_op jit(solution)/shard_map/ppermute | solution.py:23
  103.3 51.8 %copy-start.1 = (bf16[192,27,192]{2,0,1:T(8,128)(2,1)S(1)}, bf16[192,27,192]{2,0,1:T(8,128)(2,1)}, u32[]{:S(2)}) copy-start(bf16[192,27,192]{2,0,1:T(8,128)(2,1)} %param.8) | copy-start | bytes 5971972

commit v3 on v2

--- a/solution.py
+++ b/solution.py
@@ -25,12 +25,7 @@
     return block
 
 
-def silu_slope(v):
-    sigma = jax.nn.sigmoid(v)
-    return sigma * (1.0 + v * (1.0 - sigma))
-
-
-def columns_of(bricks, start, flip):
+def window_of(bricks, start):
     channels = bricks.shape[1]
     cube = bricks.reshape(BE, BE, BE, channels)
     zero = jnp.zeros((), jnp.int32)
@@ -40,19 +35,88 @@
     window = lax.dynamic_slice(
         wide, (start[0], start[1], zero, zero), (BE + 2, BE + 2, BE, channels)
     )
-    window = jnp.pad(window, ((0, 0), (0, 0), (1, 1), (0, 0)))
-    pieces = []
-    for a in range(3):
-        for b in range(3):
-            for c in range(3):
-                s = (2 - a, 2 - b, 2 - c) if flip else (a, b, c)
-                view = window[s[0] : s[0] + BE, s[1] : s[1] + BE, s[2] : s[2] + BE, :]
-                pieces.append(view.reshape(BE * BE * BE, channels))
-    return jnp.concatenate(pieces, axis=1)
+    return jnp.pad(window.astype(jnp.float32), ((0, 0), (0, 0), (0, 0), (0, 256 - channels)))
+
+
+def shifted(win, zs, odd):
+    flat = win[...].reshape(800, 256)
+    row = lax.broadcasted_iota(jnp.int32, flat.shape, 0) & 7
+    below = jnp.where(row == 0, 0.0, pltpu.roll(flat, 1, 0))
+    above = jnp.where(row == 7, 0.0, pltpu.roll(flat, 799, 0))
+    for c, value in enumerate((below, flat, above)):
+        zs[c] = value.reshape(10, 10, 8, 256)
+        odd[c] = pltpu.roll(value, 64, 1).reshape(10, 10, 8, 256)
+
+
+def tap_view(ref, tap, flip):
+    a, b, c = tap // 9, tap // 3 % 3, tap % 3
+    if flip:
+        a, b, c = 2 - a, 2 - b, 2 - c
+    return ref[c, a : a + BE, b : b + BE].reshape(512, 256)
+
+
+def fill_columns(cols, zs, odd, flip):
+    for pair in range(HALF):
+        at = 384 * pair
+        even = tap_view(zs, 2 * pair, flip)
+        cols[:, at : at + 128] = even[:, :128].astype(jnp.bfloat16)
+        if pair < HALF - 1:
+            late = tap_view(odd, 2 * pair + 1, flip)
+            cols[:, at + 128 : at + 256] = (even[:, 128:] + late[:, :128]).astype(jnp.bfloat16)
+            cols[:, at + 256 : at + 384] = late[:, 128:].astype(jnp.bfloat16)
+        else:
+            cols[:, at + 128 : at + 256] = even[:, 128:].astype(jnp.bfloat16)
+            cols[:, at + 256 : at + 384] = jnp.zeros((512, 128), jnp.bfloat16)
+
+
+def dot_nt(left, right):
+    return lax.dot_general(
+        left, right, (((1,), (1,)), ((), ())), preferred_element_type=jnp.float32
+    )
+
+
+def forward_kernel(win, w_fwd, cot, mask, output, g_out, part, zs, odd, cols):
+    shifted(win, zs, odd)
+    fill_columns(cols, zs, odd, False)
+    pre = dot_nt(w_fwd[...], cols[...])
+    sigma = 1.0 / (1.0 + jnp.exp(-pre))
+    keep = mask[...]
+    output[...] = (pre * sigma * keep).astype(jnp.bfloat16)
+    slope = sigma * (1.0 + pre * (1.0 - sigma))
+    g = (cot[...].astype(jnp.float32) * slope * keep).astype(jnp.bfloat16)
+    g_out[...] = g
+    depth = part.shape[3]
+    for h in range(2):
+        grad = jnp.dot(
+            g, cols[:, depth * h : depth * h + depth], preferred_element_type=jnp.float32
+        )
+        part[h] = grad.astype(jnp.bfloat16).reshape(part.shape[1:])
+
+
+VMEM_SPEC = pl.BlockSpec(memory_space=pltpu.VMEM)
+SHIFT_SCRATCH = [
+    pltpu.VMEM((3, 10, 10, 8, 256), jnp.float32),
+    pltpu.VMEM((3, 10, 10, 8, 256), jnp.float32),
+    pltpu.VMEM((512, 384 * HALF), jnp.bfloat16),
+]
+
+
+def forward(win, w_fwd, cot, mask):
+    channels, voxels = cot.shape
+    plane = jax.ShapeDtypeStruct((channels, voxels), jnp.bfloat16)
+    return pl.pallas_call(
+        forward_kernel,
+        out_shape=(
+            plane, plane, jax.ShapeDtypeStruct((2, 4, 48, HALF * channels), jnp.bfloat16)
+        ),
+        in_specs=[VMEM_SPEC] * 4,
+        out_specs=(VMEM_SPEC,) * 3,
+        scratch_shapes=SHIFT_SCRATCH,
+    )(win, w_fwd, cot, mask)
 
 
 def scatter_kernel(
-    part, out, core_rx, mid, x_rx, acc, yb, y_rx, flat, rows, turned, zb, z_rx,
+    part, win, w_bwd, mask, out, x_grad, zs, odd, cols, core_rx, mid, x_rx, acc, yb, y_rx, flat, rows, turned, zb, z_rx,
     core_send, core_recv, x_send, x_recv, y_send, y_recv, z_send, z_recv, fin_send, fin_recv,
 ):
     gx, gy = lax.axis_index("gx"), lax.axis_index("gy")
@@ -102,6 +166,9 @@
             x_copy[k].start()
         else:
             acc[0:48, :] = total
+    shifted(win, zs, odd)
+    fill_columns(cols, zs, odd, True)
+    x_grad[...] = (dot_nt(w_bwd[...], cols[...]) * mask[...]).astype(jnp.bfloat16)
     for k in (1, 3, 2):
         x_copy[k].wait_recv()
         acc[0:48, :] += x_rx[k - 1].astype(jnp.float32)
@@ -147,16 +214,16 @@
     last.wait()
 
 
-def scattered(part):
+def scattered(part, win, w_bwd, mask):
     depth = part.shape[3]
     bf, f32 = jnp.bfloat16, jnp.float32
     dma = pltpu.SemaphoreType.DMA
     return pl.pallas_call(
         scatter_kernel,
-        out_shape=jax.ShapeDtypeStruct((2, 16, 256), f32),
-        in_specs=[pl.BlockSpec(memory_space=pltpu.VMEM)],
-        out_specs=pl.BlockSpec(memory_space=pltpu.VMEM),
-        scratch_shapes=[
+        out_shape=(jax.ShapeDtypeStruct((2, 16, 256), f32), jax.ShapeDtypeStruct((192, 512), bf)),
+        in_specs=[VMEM_SPEC] * 4,
+        out_specs=(VMEM_SPEC,) * 2,
+        scratch_shapes=SHIFT_SCRATCH + [
             pltpu.VMEM((4, 48, depth), bf),
             pltpu.VMEM((4, 48, depth), bf),
             pltpu.VMEM((3, 48, depth), bf),
@@ -172,7 +239,7 @@
             dma((15,)), dma((15,)), dma, dma,
         ],
         compiler_params=pltpu.CompilerParams(collective_id=0, has_side_effects=True),
-    )(part)
+    )(part, win, w_bwd, mask)
 
 
 def shards(features, occupancy, brick_pos, weight, cotangent):
@@ -181,24 +248,13 @@
     mask = occupancy[0, 0].astype(jnp.bfloat16)
     pos = brick_pos[0, 0, 0]
     start = (pos // TY * BE, pos % TY * BE)
-    xm = (x * mask).T
-    cols = columns_of(xm, start, False)
-    w_fwd = weight.reshape(channels, 27 * channels)
-    pre = jnp.einsum("ok,vk->ov", w_fwd, cols, preferred_element_type=jnp.float32)
+    win = window_of((x * mask).T, start)
     maskf = mask.astype(jnp.float32)
-    output = (jax.nn.silu(pre) * maskf).astype(jnp.bfloat16)
-    g = (cotangent[0, 0, 0].astype(jnp.float32) * silu_slope(pre) * maskf).astype(jnp.bfloat16)
-    gcols = columns_of(g.T, start, True)
-    cut = HALF * channels
-    low = jnp.einsum("ov,vk->ok", g, cols[:, :cut], preferred_element_type=jnp.float32)
-    high = jnp.einsum("ov,vk->ok", g, cols[:, cut:], preferred_element_type=jnp.float32)
-    high = jnp.pad(high, ((0, 0), (0, 2 * cut - 27 * channels)))
-    part = jnp.stack([low, high]).astype(jnp.bfloat16).reshape(2, 4, 48, cut)
-    part, gcols = lax.optimization_barrier((part, gcols))
-    w_bwd = weight.transpose(1, 0, 2).reshape(27 * channels, channels)
-    back = jnp.einsum("ki,vk->iv", w_bwd, gcols, preferred_element_type=jnp.float32)
-    x_grad = (back * maskf).astype(jnp.bfloat16)
-    total = scattered(part)
+    tail = ((0, 0), (0, channels))
+    w_fwd = jnp.pad(weight.reshape(channels, 27 * channels), tail)
+    w_bwd = jnp.pad(weight.transpose(2, 1, 0).reshape(channels, 27 * channels), tail)
+    output, g, part = forward(win, w_fwd, cotangent[0, 0, 0], maskf)
+    total, x_grad = scattered(part, window_of(g.T, start), w_bwd, maskf)
     mine = lax.dynamic_slice(total, (0, lax.axis_index("gy") % 2 * 6, 0), (2, 6, 16 * HALF))
     mine = mine.reshape(2, 6, HALF, 16)[:, :, :, :12].transpose(3, 0, 2, 1)
     w_grad = mine.reshape(12, 2 * HALF, 6)[:, :27] / (lax.axis_size("gx") * lax.axis_size("gy"))

time: 163 us -> 130 us (0.80); the launches traced: 160 us -> 129 us
  local copies, waits for them, and re-layouts: 42.8 us -> 21.5 us
  matrix products: 15.4 us -> 0 us
  waiting for transfers between devices: 14.2 us -> 4.72 us
  Pallas kernels: 50 us -> 58.2 us
  starting transfers between devices: 31.4 us -> 37.9 us
    concatenate x4 -> x0, local copies, waits for them, and re-layouts: 31.6 us -> none  [columns_of(): return jnp.concatenate(pieces, axis=1)]
    dot_general x4 -> x0, matrix products: 15.4 us -> none  [the longest x1 6.1 us: shards(): jnp.einsum('ok,vk->ov', w_fwd, cols, preferred_element_type=jnp.float32)]
    ppermute x4, waiting for transfers between devices: 12.9 us -> 2.11 us  [extended(): lax.ppermute(lax.slice_in_dim(block, 0, width, axis=dim), axis, backward)]
    pallas_call x1 -> x2, Pallas kernels: 50 us -> 58.2 us  [the longest x1 51.6 us: scattered(): pl.pallas_call(scatter_kernel, out_shape=(jax.ShapeDtypeStruct((2, 16, 25...]
    reshape x0 -> x2, local copies, waits for them, and re-layouts: none -> 7.66 us  [the longest x1 4.32 us: shards(): w_fwd = jnp.pad(weight.reshape(channels, 27 * channels), tail)]
    ppermute x4, starting transfers between devices: 22.7 us -> 28.9 us  [extended(): lax.ppermute(lax.slice_in_dim(block, block.shape[dim] - width, None, axis...]
    pad x1 -> x2, local copies, waits for them, and re-layouts: 0.08 us -> 6.18 us  [the longest x1 3.09 us: shards(): jnp.pad(weight.transpose(2, 1, 0).reshape(channels, 27 * channels), tail)]
    slice x4 -> x0, local copies, waits for them, and re-layouts: 5.01 us -> none  [columns_of(): view = window[s[0]:s[0] + BE, s[1]:s[1] + BE, s[2]:s[2] + BE, :]]
  transfers between devices with their start and end apart: 8 -> 8, of which waited for: 3 -> 3; matrix products, arithmetic and copies ran while one was open for 5% -> 14% of each run, Pallas kernels for 0% -> 0%
where the time goes in v3:
time: 130 us; the launch traced here: 129 us
  Pallas kernels  58.2 us (45%)
  starting transfers between devices  37.9 us (29%)
  local copies, waits for them, and re-layouts  21.5 us (17%)
  other arithmetic  5.44 us (4%)
  waiting for transfers between devices  4.72 us (4%)
  between operations  1.58 us (1%)
    pallas_call x1, Pallas kernels, scattered(): pl.pallas_call(scatter_kernel, out_shape=(jax.ShapeDtypeStruct((2, 16, 25...  51.6 us
    ppermute x4, starting transfers between devices, extended(): lax.ppermute(lax.slice_in_dim(block, block.shape[dim] - width, None, axis...  28.9 us
    ppermute x4, starting transfers between devices, extended(): lax.ppermute(lax.slice_in_dim(block, 0, width, axis=dim), axis, backward)  9 us
    pallas_call x1, Pallas kernels, forward(): pl.pallas_call(forward_kernel, out_shape=(plane, plane, jax.ShapeDtypeStr...  6.67 us
    unnamed x14, local copies, waits for them, and re-layouts  5.04 us
    reshape x1, local copies, waits for them, and re-layouts, shards(): w_fwd = jnp.pad(weight.reshape(channels, 27 * channels), tail)  4.32 us
    reshape x1, local copies, waits for them, and re-layouts, shards(): weight.transpose(2, 1, 0).reshape(channels, 27 * channels)  3.34 us
    pad x1, local copies, waits for them, and re-layouts, shards(): jnp.pad(weight.transpose(2, 1, 0).reshape(channels, 27 * channels), tail)  3.09 us
  transfers between devices with their start and end apart: 8, of which 3 were waited for; matrix products, arithmetic and copies ran while one was open for 14% of the time, Pallas kernels for 0%

profile of v3, /device:TPU:57, one launch (start us, length us, event | category | flops | bytes accessed | tf_op | source)
XLA Modules:
  0.0 129.4 jit_solution(3871284180114225634)
XLA Ops:
  1.3 0.7 convert_reduce_fusion
  2.0 0.9 fusion.8
  3.0 0.1 copy.19
  3.1 0.0 copy-start.5
  3.1 0.0 copy-start
  3.1 0.1 broadcast.15.clone
  3.3 0.0 copy-start.3
  3.3 3.2 %collective-permute-start.1 = (bf16[1,16,8,192]{3,2,1,0:T(8,128)(2,1)S(1)}, bf16[1,16,8,192]{3,2,1,0:T(8,128)(2,1)S(1)}, u32[]{:S(2)}, u32[]{:S(2)}) collective-permute-start(bf16[1,16,8,192]{3,2,1,0:T(8,128)(2,1)S(1)} %get-tuple-element.20), channel_id=1, source_target_pairs={{32,0},{64,32},{96,64},{128,96},{160,128},{192,160},{224,192},{256... | collective-permute-start | bytes 147464 | tf_op jit(solution)/shard_map/ppermute | solution.py:23
  6.5 5.0 %collective-permute-start = (bf16[1,16,8,192]{3,2,1,0:T(8,128)(2,1)S(1)}, bf16[1,16,8,192]{3,2,1,0:T(8,128)(2,1)S(1)}, u32[]{:S(2)}, u32[]{:S(2)}) collective-permute-start(bf16[1,16,8,192]{3,2,1,0:T(8,128)(2,1)S(1)} %get-tuple-element.19), channel_id=1, source_target_pairs={{0,32},{32,64},{64,96},{96,128},{128,160},{160,192},{192,224},{224... | collective-permute-start | bytes 147464 | tf_op jit(solution)/shard_map/ppermute | solution.py:20
  11.6 0.0 collective-permute-done.1
  11.6 1.3 %collective-permute-done = bf16[1,16,8,192]{3,2,1,0:T(8,128)(2,1)S(1)} collective-permute-done((bf16[1,16,8,192]{3,2,1,0:T(8,128)(2,1)S(1)}, bf16[1,16,8,192]{3,2,1,0:T(8,128)(2,1)S(1)}, u32[]{:S(2)}, u32[]{:S(2)}) %collective-permute-start) | collective-permute-done | bytes 49184 | tf_op jit(solution)/shard_map/ppermute | solution.py:20
  12.9 0.0 copy-done.3
  12.9 7.9 %collective-permute-start.2 = (bf16[18,1,8,192]{3,2,1,0:T(8,128)(2,1)S(1)}, bf16[18,1,8,192]{3,2,1,0:T(8,128)(2,1)S(1)}, u32[]{:S(2)}, u32[]{:S(2)}) collective-permute-start(bf16[18,1,8,192]{3,2,1,0:T(8,128)(2,1)S(1)} %get-tuple-element.16), channel_id=1, source_target_pairs={{0,1},{1,2},{2,3},{3,4},{4,5},{5,6},{6,7},{7,8},{8,9},{9,10},{10,1... | collective-permute-start | bytes 165896 | tf_op jit(solution)/shard_map/ppermute | solution.py:20
  20.9 1.9 %collective-permute-start.3 = (bf16[18,1,8,192]{3,2,1,0:T(8,128)(2,1)S(1)}, bf16[18,1,8,192]{3,2,1,0:T(8,128)(2,1)S(1)}, u32[]{:S(2)}, u32[]{:S(2)}) collective-permute-start(bf16[18,1,8,192]{3,2,1,0:T(8,128)(2,1)S(1)} %get-tuple-element.15), channel_id=1, source_target_pairs={{1,0},{2,1},{3,2},{4,3},{5,4},{6,5},{7,6},{8,7},{9,8},{10,9},{11,1... | collective-permute-start | bytes 165896 | tf_op jit(solution)/shard_map/ppermute | solution.py:23
  22.8 0.0 copy-done.5
  22.8 0.6 bitcast_convert_fusion.mask
  23.4 0.0 copy-done
  23.4 3.4 %copy.20 = bf16[192,27,192]{0,2,1:T(8,128)(2,1)} copy(bf16[192,27,192]{2,0,1:T(8,128)(2,1)S(1)} %copy-done) | data formatting | bytes 3981312 | tf_op args[3]
  26.8 4.3 %copy.21 = bf16[192,5184]{1,0:T(8,128)(2,1)} copy(bf16[192,5184]{0,1:T(8,128)(2,1)} %bitcast.31) | data formatting | bytes 3981312 | tf_op jit(solution)/shard_map/reshape | solution.py:254
  31.1 3.1 %pad.20.w_fwd = bf16[192,5376]{1,0:T(8,128)(2,1)} pad(bf16[192,5184]{1,0:T(8,128)(2,1)} %copy.21, bf16[]{:T(256)} %constant.38.clone.1), padding=0_0x0_192 | pad | bytes 4055042 | tf_op jit(solution)/shard_map/jit(_pad)/pad | solution.py:254
  34.2 0.0 collective-permute-done.2
  34.2 0.0 collective-permute-done.3
  34.2 0.3 fusion.5
  34.5 1.0 pad_convert_fusion.1.win
  35.5 6.7 %shard_map.76 = (bf16[192,512]{1,0:T(8,128)(2,1)}, bf16[192,512]{1,0:T(8,128)(2,1)}, bf16[2,4,48,2688]{3,2,1,0:T(8,128)(2,1)}) custom-call(f32[10,10,8,256]{3,2,1,0:T(8,128)} %pad_convert_fusion.1.win, bf16[192,5376]{1,0:T(8,128)(2,1)} %pad.20.w_fwd, bf16[192,512]{1,0:T(8,128)(2,1)} %bitcast.36, f32[1,512]{1,0:T(1,128)} %bitcast_convert_fusion.mask), custom_call_target="tpu_custom_call" | custom-call | tf_op jit(solution)/shard_map/pallas_call | solution.py:107
  42.1 1.1 copy.22
  43.2 0.1 broadcast.15
  43.3 0.0 copy-start.1
  43.4 1.9 %collective-permute-start.5 = (bf16[1,16,8,192]{3,2,1,0:T(8,128)(2,1)S(1)}, bf16[1,16,8,192]{3,2,1,0:T(8,128)(2,1)S(1)}, u32[]{:S(2)}, u32[]{:S(2)}) collective-permute-start(bf16[1,16,8,192]{3,2,1,0:T(8,128)(2,1)S(1)} %get-tuple-element.18), channel_id=1, source_target_pairs={{32,0},{64,32},{96,64},{128,96},{160,128},{192,160},{224,192},{256... | collective-permute-start | bytes 147464 | tf_op jit(solution)/shard_map/ppermute | solution.py:23
  45.3 6.7 %collective-permute-start.4 = (bf16[1,16,8,192]{3,2,1,0:T(8,128)(2,1)S(1)}, bf16[1,16,8,192]{3,2,1,0:T(8,128)(2,1)S(1)}, u32[]{:S(2)}, u32[]{:S(2)}) collective-permute-start(bf16[1,16,8,192]{3,2,1,0:T(8,128)(2,1)S(1)} %get-tuple-element.17), channel_id=1, source_target_pairs={{0,32},{32,64},{64,96},{96,128},{128,160},{160,192},{192,224},{224... | collective-permute-start | bytes 147464 | tf_op jit(solution)/shard_map/ppermute | solution.py:20
  52.0 0.0 collective-permute-done.5
  52.0 1.3 %collective-permute-done.4 = bf16[1,16,8,192]{3,2,1,0:T(8,128)(2,1)S(1)} collective-permute-done((bf16[1,16,8,192]{3,2,1,0:T(8,128)(2,1)S(1)}, bf16[1,16,8,192]{3,2,1,0:T(8,128)(2,1)S(1)}, u32[]{:S(2)}, u32[]{:S(2)}) %collective-permute-start.4) | collective-permute-done | bytes 49184 | tf_op jit(solution)/shard_map/ppermute | solution.py:20
  53.3 0.0 copy-done.1
  53.3 9.3 %collective-permute-start.6 = (bf16[18,1,8,192]{3,2,1,0:T(8,128)(2,1)S(1)}, bf16[18,1,8,192]{3,2,1,0:T(8,128)(2,1)S(1)}, u32[]{:S(2)}, u32[]{:S(2)}) collective-permute-start(bf16[18,1,8,192]{3,2,1,0:T(8,128)(2,1)S(1)} %get-tuple-element.14), channel_id=1, source_target_pairs={{0,1},{1,2},{2,3},{3,4},{4,5},{5,6},{6,7},{7,8},{8,9},{9,10},{10,1... | collective-permute-start | bytes 165896 | tf_op jit(solution)/shard_map/ppermute | solution.py:20
  62.7 1.9 %collective-permute-start.7 = (bf16[18,1,8,192]{3,2,1,0:T(8,128)(2,1)S(1)}, bf16[18,1,8,192]{3,2,1,0:T(8,128)(2,1)S(1)}, u32[]{:S(2)}, u32[]{:S(2)}) collective-permute-start(bf16[18,1,8,192]{3,2,1,0:T(8,128)(2,1)S(1)} %get-tuple-element.13), channel_id=1, source_target_pairs={{1,0},{2,1},{3,2},{4,3},{5,4},{6,5},{7,6},{8,7},{9,8},{10,9},{11,1... | collective-permute-start | bytes 165896 | tf_op jit(solution)/shard_map/ppermute | solution.py:23
  64.6 3.3 %copy.23 = bf16[192,5184]{1,0:T(8,128)(2,1)} copy(bf16[192,5184]{0,1:T(8,128)(2,1)S(1)} %bitcast.30) | data formatting | bytes 3981312 | tf_op jit(solution)/shard_map/reshape | solution.py:255
  67.9 3.1 %pad.23.w_bwd = bf16[192,5376]{1,0:T(8,128)(2,1)} pad(bf16[192,5184]{1,0:T(8,128)(2,1)} %copy.23, bf16[]{:T(256)} %constant.38.clone.1), padding=0_0x0_192 | pad | bytes 4055042 | tf_op jit(solution)/shard_map/jit(_pad)/pad | solution.py:255
  71.0 0.0 collective-permute-done.6
  71.0 2.1 %collective-permute-done.7 = bf16[18,1,8,192]{3,2,1,0:T(8,128)(2,1)S(1)} collective-permute-done((bf16[18,1,8,192]{3,2,1,0:T(8,128)(2,1)S(1)}, bf16[18,1,8,192]{3,2,1,0:T(8,128)(2,1)S(1)}, u32[]{:S(2)}, u32[]{:S(2)}) %collective-permute-start.7) | collective-permute-done | bytes 55328 | tf_op jit(solution)/shard_map/ppermute | solution.py:23
  73.1 0.3 fusion.1
  73.4 1.0 pad_convert_fusion.win
  74.4 51.6 %shard_map.77 = (f32[2,16,256]{2,1,0:T(8,128)}, bf16[192,512]{1,0:T(8,128)(2,1)}) custom-call(bf16[2,4,48,2688]{3,2,1,0:T(8,128)(2,1)} %get-tuple-element.9.part, f32[10,10,8,256]{3,2,1,0:T(8,128)} %pad_convert_fusion.win, bf16[192,5376]{1,0:T(8,128)(2,1)} %pad.23.w_bwd, f32[1,512]{1,0:T(1,128)} %bitcast_convert_fusion.mask), custom_call_target="tpu_custom_call" | custom-call | tf_op jit(solution)/shard_map/pallas_call | solution.py:221
  126.0 0.8 constant_dynamic-slice_fusion
  126.8 0.1 reshape.51
  126.9 0.2 copy.25
  127.0 0.1 reshape.52
  127.1 0.6 slice_multiply_fusion
  127.8 1.6 %copy.32 = bf16[1,1,1,192,512]{4,3,2,1,0:T(8,128)(2,1)} copy(bf16[1,1,1,192,512]{4,3,2,1,0:T(8,128)(2,1)} %bitcast.35) | data formatting | bytes 393216
  (12 shorter events, 0.2 us)
Async XLA Ops:
  3.1 19.7 %copy-start.5 = (s32[1,1,1,512]{3,2,1,0:T(1,128)S(1)}, s32[1,1,1,512]{3,2,1,0:T(1,128)}, u32[]{:S(2)}) copy-start(s32[1,1,1,512]{3,2,1,0:T(1,128)} %param.6) | copy-start | bytes 6148
  3.1 20.3 %copy-start = (bf16[192,27,192]{2,0,1:T(8,128)(2,1)S(1)}, bf16[192,27,192]{2,0,1:T(8,128)(2,1)}, u32[]{:S(2)}) copy-start(bf16[192,27,192]{2,0,1:T(8,128)(2,1)} %param.8) | copy-start | bytes 5971972
  3.3 9.6 %copy-start.3 = (bf16[16,16,8,192]{3,2,1,0:T(8,128)(2,1)}, bf16[16,16,8,192]{3,2,1,0:T(8,128)(2,1)S(1)}, u32[]{:S(2)}) copy-start(bf16[16,16,8,192]{3,2,1,0:T(8,128)(2,1)S(1)} %constant_dynamic-update-slice_fusion.1) | copy-start | bytes 2359300
  3.3 8.3 %collective-permute-start.1 = (bf16[1,16,8,192]{3,2,1,0:T(8,128)(2,1)S(1)}, bf16[1,16,8,192]{3,2,1,0:T(8,128)(2,1)S(1)}, u32[]{:S(2)}, u32[]{:S(2)}) collective-permute-start(bf16[1,16,8,192]{3,2,1,0:T(8,128)(2,1)S(1)} %get-tuple-element.20), channel_id=1, source_target_pairs={{32,0},{64,32},{96,64},{128,96},{160,128},{192,160},{224,192},{256... | collective-permute-start | bytes 147464 | tf_op jit(solution)/shard_map/ppermute | solution.py:23
  6.5 6.3 %collective-permute-start = (bf16[1,16,8,192]{3,2,1,0:T(8,128)(2,1)S(1)}, bf16[1,16,8,192]{3,2,1,0:T(8,128)(2,1)S(1)}, u32[]{:S(2)}, u32[]{:S(2)}) collective-permute-start(bf16[1,16,8,192]{3,2,1,0:T(8,128)(2,1)S(1)} %get-tuple-element.19), channel_id=1, source_target_pairs={{0,32},{32,64},{64,96},{96,128},{128,160},{160,192},{192,224},{224... | collective-permute-start | bytes 147464 | tf_op jit(solution)/shard_map/ppermute | solution.py:20
  12.9 21.3 %collective-permute-start.2 = (bf16[18,1,8,192]{3,2,1,0:T(8,128)(2,1)S(1)}, bf16[18,1,8,192]{3,2,1,0:T(8,128)(2,1)S(1)}, u32[]{:S(2)}, u32[]{:S(2)}) collective-permute-start(bf16[18,1,8,192]{3,2,1,0:T(8,128)(2,1)S(1)} %get-tuple-element.16), channel_id=1, source_target_pairs={{0,1},{1,2},{2,3},{3,4},{4,5},{5,6},{6,7},{7,8},{8,9},{9,10},{10,1... | collective-permute-start | bytes 165896 | tf_op jit(solution)/shard_map/ppermute | solution.py:20
  20.9 13.3 %collective-permute-start.3 = (bf16[18,1,8,192]{3,2,1,0:T(8,128)(2,1)S(1)}, bf16[18,1,8,192]{3,2,1,0:T(8,128)(2,1)S(1)}, u32[]{:S(2)}, u32[]{:S(2)}) collective-permute-start(bf16[18,1,8,192]{3,2,1,0:T(8,128)(2,1)S(1)} %get-tuple-element.15), channel_id=1, source_target_pairs={{1,0},{2,1},{3,2},{4,3},{5,4},{6,5},{7,6},{8,7},{9,8},{10,9},{11,1... | collective-permute-start | bytes 165896 | tf_op jit(solution)/shard_map/ppermute | solution.py:23
  31.1 3.1 %copy-start.4 = (bf16[16,16,8,192]{3,2,1,0:T(8,128)(2,1)S(1)}, bf16[16,16,8,192]{3,2,1,0:T(8,128)(2,1)}, u32[]{:S(2)}) copy-start(bf16[16,16,8,192]{3,2,1,0:T(8,128)(2,1)} %copy-done.3) | copy-start | bytes 2359300
  43.3 10.0 %copy-start.1 = (bf16[16,16,8,192]{3,2,1,0:T(8,128)(2,1)}, bf16[16,16,8,192]{3,2,1,0:T(8,128)(2,1)S(1)}, u32[]{:S(2)}) copy-start(bf16[16,16,8,192]{3,2,1,0:T(8,128)(2,1)S(1)} %constant_dynamic-update-slice_fusion) | copy-start | bytes 2359300
  43.4 8.6 %collective-permute-start.5 = (bf16[1,16,8,192]{3,2,1,0:T(8,128)(2,1)S(1)}, bf16[1,16,8,192]{3,2,1,0:T(8,128)(2,1)S(1)}, u32[]{:S(2)}, u32[]{:S(2)}) collective-permute-start(bf16[1,16,8,192]{3,2,1,0:T(8,128)(2,1)S(1)} %get-tuple-element.18), channel_id=1, source_target_pairs={{32,0},{64,32},{96,64},{128,96},{160,128},{192,160},{224,192},{256... | collective-permute-start | bytes 147464 | tf_op jit(solution)/shard_map/ppermute | solution.py:23
  45.3 8.0 %collective-permute-start.4 = (bf16[1,16,8,192]{3,2,1,0:T(8,128)(2,1)S(1)}, bf16[1,16,8,192]{3,2,1,0:T(8,128)(2,1)S(1)}, u32[]{:S(2)}, u32[]{:S(2)}) collective-permute-start(bf16[1,16,8,192]{3,2,1,0:T(8,128)(2,1)S(1)} %get-tuple-element.17), channel_id=1, source_target_pairs={{0,32},{32,64},{64,96},{96,128},{128,160},{160,192},{192,224},{224... | collective-permute-start | bytes 147464 | tf_op jit(solution)/shard_map/ppermute | solution.py:20
  53.3 17.7 %collective-permute-start.6 = (bf16[18,1,8,192]{3,2,1,0:T(8,128)(2,1)S(1)}, bf16[18,1,8,192]{3,2,1,0:T(8,128)(2,1)S(1)}, u32[]{:S(2)}, u32[]{:S(2)}) collective-permute-start(bf16[18,1,8,192]{3,2,1,0:T(8,128)(2,1)S(1)} %get-tuple-element.14), channel_id=1, source_target_pairs={{0,1},{1,2},{2,3},{3,4},{4,5},{5,6},{6,7},{7,8},{8,9},{9,10},{10,1... | collective-permute-start | bytes 165896 | tf_op jit(solution)/shard_map/ppermute | solution.py:20
  62.7 10.5 %collective-permute-start.7 = (bf16[18,1,8,192]{3,2,1,0:T(8,128)(2,1)S(1)}, bf16[18,1,8,192]{3,2,1,0:T(8,128)(2,1)S(1)}, u32[]{:S(2)}, u32[]{:S(2)}) collective-permute-start(bf16[18,1,8,192]{3,2,1,0:T(8,128)(2,1)S(1)} %get-tuple-element.13), channel_id=1, source_target_pairs={{1,0},{2,1},{3,2},{4,3},{5,4},{6,5},{7,6},{8,7},{9,8},{10,9},{11,1... | collective-permute-start | bytes 165896 | tf_op jit(solution)/shard_map/ppermute | solution.py:23
  67.9 5.2 %copy-start.2 = (bf16[16,16,8,192]{3,2,1,0:T(8,128)(2,1)S(1)}, bf16[16,16,8,192]{3,2,1,0:T(8,128)(2,1)}, u32[]{:S(2)}) copy-start(bf16[16,16,8,192]{3,2,1,0:T(8,128)(2,1)} %copy-done.1) | copy-start | bytes 2359300

commit v4 on v3

--- a/solution.py
+++ b/solution.py
@@ -8,34 +8,7 @@
 MESH = pl.DeviceIdType.MESH
 HALF = 14
 BE = 8
-TX = 2
 TY = 2
-
-
-def extended(block, sides, width):
-    for axis, dim in sides:
-        count = lax.axis_size(axis)
-        forward = [(i, i + 1) for i in range(count - 1)]
-        backward = [(target, source) for source, target in forward]
-        low = lax.ppermute(
-            lax.slice_in_dim(block, block.shape[dim] - width, None, axis=dim), axis, forward
-        )
-        high = lax.ppermute(lax.slice_in_dim(block, 0, width, axis=dim), axis, backward)
-        block = jnp.concatenate([low, block, high], axis=dim)
-    return block
-
-
-def window_of(bricks, start):
-    channels = bricks.shape[1]
-    cube = bricks.reshape(BE, BE, BE, channels)
-    zero = jnp.zeros((), jnp.int32)
-    lattice = jnp.zeros((TX * BE, TY * BE, BE, channels), bricks.dtype)
-    lattice = lax.dynamic_update_slice(lattice, cube, (start[0], start[1], zero, zero))
-    wide = extended(lattice, (("gx", 0), ("gy", 1)), 1)
-    window = lax.dynamic_slice(
-        wide, (start[0], start[1], zero, zero), (BE + 2, BE + 2, BE, channels)
-    )
-    return jnp.pad(window.astype(jnp.float32), ((0, 0), (0, 0), (0, 0), (0, 256 - channels)))
 
 
 def shifted(win, zs, odd):
@@ -75,48 +48,49 @@
     )
 
 
-def forward_kernel(win, w_fwd, cot, mask, output, g_out, part, zs, odd, cols):
-    shifted(win, zs, odd)
-    fill_columns(cols, zs, odd, False)
-    pre = dot_nt(w_fwd[...], cols[...])
-    sigma = 1.0 / (1.0 + jnp.exp(-pre))
-    keep = mask[...]
-    output[...] = (pre * sigma * keep).astype(jnp.bfloat16)
-    slope = sigma * (1.0 + pre * (1.0 - sigma))
-    g = (cot[...].astype(jnp.float32) * slope * keep).astype(jnp.bfloat16)
-    g_out[...] = g
-    depth = part.shape[3]
-    for h in range(2):
-        grad = jnp.dot(
-            g, cols[:, depth * h : depth * h + depth], preferred_element_type=jnp.float32
+def halo_sends(own, coef, face_tx, line_tx):
+    grid = own.reshape(BE, BE, BE, 256)
+    faces = (grid[7], grid[0], grid[:, 7], grid[:, 0])
+    for d, face in enumerate(faces):
+        flat = face.reshape(64, 256)
+        both = jnp.concatenate(
+            [flat * coef[2 * d : 2 * d + 1, :], flat * coef[2 * d + 1 : 2 * d + 2, :]], axis=0
         )
-        part[h] = grad.astype(jnp.bfloat16).reshape(part.shape[1:])
+        face_tx[d] = both.astype(jnp.bfloat16)
+    lines = (grid[7, 7], grid[7, 0], grid[0, 7], grid[0, 0])
+    for d, line in enumerate(lines):
+        line = line * coef[8 + d : 9 + d, :]
+        line_tx[d] = jnp.concatenate([line, jnp.zeros_like(line)], axis=0).astype(jnp.bfloat16)
+
+
+def fill_ring(win, coef, face_rx, line_rx):
+    px0, px1, py0, py1 = (coef[12 + d : 13 + d, :] for d in range(4))
+    xm, xp, ym, yp = (
+        face_rx[d].astype(jnp.float32).reshape(16, BE, 256) for d in range(4)
+    )
+    mm, mp, pm, pp = (line_rx[d].astype(jnp.float32)[:BE] for d in range(4))
+    win[0, 1:9] = px0 * (py0 * xm[:8] + py1 * xm[8:])
+    win[9, 1:9] = px1 * (py0 * xp[:8] + py1 * xp[8:])
+    win[1:9, 0] = py0 * (px0 * ym[:8] + px1 * ym[8:])
+    win[1:9, 9] = py1 * (px0 * yp[:8] + px1 * yp[8:])
+    win[0, 0] = py0 * (px0 * mm + px1 * ym[7]) + py1 * (px0 * xm[7])
+    win[9, 0] = py0 * (px0 * ym[8] + px1 * pm) + py1 * (px1 * xp[7])
+    win[0, 9] = py1 * (px0 * mp + px1 * yp[7]) + py0 * (px0 * xm[8])
+    win[9, 9] = py1 * (px0 * yp[8] + px1 * pp) + py0 * (px1 * xp[8])
+
+
+def voxel_major(value):
+    channels, voxels = value.shape
+    return jnp.concatenate([value, jnp.zeros((256 - channels, voxels), jnp.float32)], axis=0).T
 
 
 VMEM_SPEC = pl.BlockSpec(memory_space=pltpu.VMEM)
-SHIFT_SCRATCH = [
-    pltpu.VMEM((3, 10, 10, 8, 256), jnp.float32),
-    pltpu.VMEM((3, 10, 10, 8, 256), jnp.float32),
-    pltpu.VMEM((512, 384 * HALF), jnp.bfloat16),
-]
-
-
-def forward(win, w_fwd, cot, mask):
-    channels, voxels = cot.shape
-    plane = jax.ShapeDtypeStruct((channels, voxels), jnp.bfloat16)
-    return pl.pallas_call(
-        forward_kernel,
-        out_shape=(
-            plane, plane, jax.ShapeDtypeStruct((2, 4, 48, HALF * channels), jnp.bfloat16)
-        ),
-        in_specs=[VMEM_SPEC] * 4,
-        out_specs=(VMEM_SPEC,) * 3,
-        scratch_shapes=SHIFT_SCRATCH,
-    )(win, w_fwd, cot, mask)
-
-
-def scatter_kernel(
-    part, win, w_bwd, mask, out, x_grad, zs, odd, cols, core_rx, mid, x_rx, acc, yb, y_rx, flat, rows, turned, zb, z_rx,
+
+
+def fused_kernel(
+    feat, cot, mask, coef, weight, output, x_grad, out, win, zs, odd, cols, packed, part,
+    face_tx, line_tx, face_rx, line_rx, core_rx, mid, x_rx, acc, yb, y_rx, flat, rows, turned,
+    zb, z_rx, face_send, face_recv, line_send, line_recv,
     core_send, core_recv, x_send, x_recv, y_send, y_recv, z_send, z_recv, fin_send, fin_recv,
 ):
     gx, gy = lax.axis_index("gx"), lax.axis_index("gy")
@@ -131,8 +105,14 @@
     y_peer = [(4 * x + y_of[k], gy) for k in range(4)]
     q_peer = [(gx, 2 * q_of[k] + core) for k in range(16)]
 
+    nx, ny = lax.axis_size("gx"), lax.axis_size("gy")
+    gx_up, gx_down = lax.rem(gx + 1, nx), lax.rem(gx + nx - 1, nx)
+    gy_up, gy_down = lax.rem(gy + 1, ny), lax.rem(gy + ny - 1, ny)
+    face_peer = [(gx_up, gy), (gx_down, gy), (gx, gy_up), (gx, gy_down)]
+    line_peer = [(gx_up, gy_up), (gx_up, gy_down), (gx_down, gy_up), (gx_down, gy_down)]
+
     barrier = pltpu.get_barrier_semaphore()
-    peers = [partner] + x_peer[1:] + y_peer[1:] + q_peer[1:]
+    peers = [partner] + x_peer[1:] + y_peer[1:] + q_peer[1:] + face_peer + line_peer
     for peer in peers:
         pl.semaphore_signal(barrier, inc=1, device_id=peer, device_id_type=MESH)
     pl.semaphore_wait(barrier, len(peers))
@@ -143,6 +123,63 @@
             device_id=peer, device_id_type=MESH,
         )
 
+    def halo(step):
+        copies = []
+        for d in range(4):
+            copies.append(
+                remote(
+                    face_tx.at[step, d], face_rx.at[step, d],
+                    face_send.at[step, d], face_recv.at[step, d], face_peer[d],
+                )
+            )
+            copies.append(
+                remote(
+                    line_tx.at[step, d], line_rx.at[step, d],
+                    line_send.at[step, d], line_recv.at[step, d], line_peer[d],
+                )
+            )
+        return copies
+
+    keep = mask[...]
+    bf, f32 = jnp.bfloat16, jnp.float32
+    channels = feat.shape[0]
+    x_halo, g_halo = halo(0), halo(1)
+    own = voxel_major(feat[...].astype(f32) * keep)
+    halo_sends(own, coef, face_tx.at[0], line_tx.at[0])
+    for copy in x_halo:
+        copy.start()
+    win[1:9, 1:9] = own.reshape(BE, BE, BE, 256)
+    for pair in range(HALF):
+        at = 2 * pair * channels
+        left = weight[at : at + channels, :]
+        if pair < HALF - 1:
+            right = weight[at + channels : at + 2 * channels, :]
+        else:
+            right = jnp.zeros((channels, channels), bf)
+        packed[:, at : at + 2 * channels] = jnp.concatenate([left, right], axis=1)
+    for copy in x_halo:
+        copy.wait_recv()
+    fill_ring(win, coef, face_rx.at[0], line_rx.at[0])
+    shifted(win, zs, odd)
+    fill_columns(cols, zs, odd, False)
+    pre = dot_nt(packed[...], cols[...])
+    sigma = 1.0 / (1.0 + jnp.exp(-pre))
+    output[...] = (pre * sigma * keep).astype(bf)
+    slope = sigma * (1.0 + pre * (1.0 - sigma))
+    g = (cot[...].astype(f32) * slope * keep).astype(bf)
+    own = voxel_major(g.astype(f32))
+    halo_sends(own, coef, face_tx.at[1], line_tx.at[1])
+    for copy in g_halo:
+        copy.start()
+    win[1:9, 1:9] = own.reshape(BE, BE, BE, 256)
+    depth = part.shape[3]
+
+    def partial(half):
+        view = cols[:, pl.ds(pl.multiple_of(half * depth, 128), depth)]
+        grad = jnp.dot(g, view, preferred_element_type=f32)
+        part[half] = grad.astype(bf).reshape(part.shape[1:])
+
+    partial(other)
     order = (2, 1, 3, 0)
     core_copy = {
         k: remote(
@@ -152,6 +189,7 @@
     }
     for k in order:
         core_copy[k].start()
+    partial(core)
     x_copy = {
         k: remote(mid.at[x_of[k]], x_rx.at[k - 1], x_send.at[k - 1], x_recv.at[k - 1], x_peer[k])
         for k in (2, 1, 3)
@@ -166,9 +204,16 @@
             x_copy[k].start()
         else:
             acc[0:48, :] = total
+    for copy in g_halo:
+        copy.wait_recv()
+    fill_ring(win, coef, face_rx.at[1], line_rx.at[1])
     shifted(win, zs, odd)
     fill_columns(cols, zs, odd, True)
-    x_grad[...] = (dot_nt(w_bwd[...], cols[...]) * mask[...]).astype(jnp.bfloat16)
+    cut, end = 26 * channels, 27 * channels
+    back = jnp.dot(cols[:, :cut], weight[:cut, :], preferred_element_type=f32)
+    back = back + jnp.dot(cols[:, cut:end], weight[cut:end, :], preferred_element_type=f32)
+    wide = jnp.concatenate([back, jnp.zeros((512, 256 - channels), f32)], axis=1)
+    x_grad[...] = (wide.T[:channels] * keep).astype(bf)
     for k in (1, 3, 2):
         x_copy[k].wait_recv()
         acc[0:48, :] += x_rx[k - 1].astype(jnp.float32)
@@ -211,19 +256,33 @@
         y_copy[k].wait_send()
     for copy in z_copy:
         copy.wait_send()
+    for copy in x_halo + g_halo:
+        copy.wait_send()
     last.wait()
 
 
-def scattered(part, win, w_bwd, mask):
-    depth = part.shape[3]
+def fused(feat, cot, mask, coef, weight):
+    channels, voxels = feat.shape
+    depth = HALF * channels
     bf, f32 = jnp.bfloat16, jnp.float32
     dma = pltpu.SemaphoreType.DMA
+    plane = jax.ShapeDtypeStruct((channels, voxels), bf)
     return pl.pallas_call(
-        scatter_kernel,
-        out_shape=(jax.ShapeDtypeStruct((2, 16, 256), f32), jax.ShapeDtypeStruct((192, 512), bf)),
-        in_specs=[VMEM_SPEC] * 4,
-        out_specs=(VMEM_SPEC,) * 2,
-        scratch_shapes=SHIFT_SCRATCH + [
+        fused_kernel,
+        out_shape=(plane, plane, jax.ShapeDtypeStruct((2, 16, 256), f32)),
+        in_specs=[VMEM_SPEC] * 5,
+        out_specs=(VMEM_SPEC,) * 3,
+        scratch_shapes=[
+            pltpu.VMEM((10, 10, BE, 256), f32),
+            pltpu.VMEM((3, 10, 10, BE, 256), f32),
+            pltpu.VMEM((3, 10, 10, BE, 256), f32),
+            pltpu.VMEM((voxels, 2 * depth), bf),
+            pltpu.VMEM((channels, 2 * depth), bf),
+            pltpu.VMEM((2, 4, 48, depth), bf),
+            pltpu.VMEM((2, 4, 128, 256), bf),
+            pltpu.VMEM((2, 4, 16, 256), bf),
+            pltpu.VMEM((2, 4, 128, 256), bf),
+            pltpu.VMEM((2, 4, 16, 256), bf),
             pltpu.VMEM((4, 48, depth), bf),
             pltpu.VMEM((4, 48, depth), bf),
             pltpu.VMEM((3, 48, depth), bf),
@@ -235,26 +294,37 @@
             pltpu.VMEM((256, 256), f32),
             pltpu.VMEM((16, 16, 256), bf),
             pltpu.VMEM((15, 16, 256), bf),
+            dma((2, 4)), dma((2, 4)), dma((2, 4)), dma((2, 4)),
             dma((4,)), dma((4,)), dma((3,)), dma((3,)), dma((3,)), dma((3,)),
             dma((15,)), dma((15,)), dma, dma,
         ],
         compiler_params=pltpu.CompilerParams(collective_id=0, has_side_effects=True),
-    )(part, win, w_bwd, mask)
+    )(feat, cot, mask, coef, weight)
+
+
+def coefficients(pos):
+    gx, gy = lax.axis_index("gx"), lax.axis_index("gy")
+    px, py = pos // TY == 1, pos % TY == 1
+    up_x, up_y = gx < lax.axis_size("gx") - 1, gy < lax.axis_size("gy") - 1
+    down_x, down_y = gx > 0, gy > 0
+    out_x, in_x = px & up_x, ~px & down_x
+    out_y, in_y = py & up_y, ~py & down_y
+    flags = [
+        out_x & ~py, out_x & py, in_x & ~py, in_x & py,
+        out_y & ~px, out_y & px, in_y & ~px, in_y & px,
+        out_x & out_y, out_x & in_y, in_x & out_y, in_x & in_y,
+        ~px, px, ~py, py,
+    ]
+    return jnp.broadcast_to(jnp.stack(flags).astype(jnp.float32)[:, None], (16, 256))
 
 
 def shards(features, occupancy, brick_pos, weight, cotangent):
-    x = features[0, 0, 0]
-    channels, voxels = x.shape
-    mask = occupancy[0, 0].astype(jnp.bfloat16)
-    pos = brick_pos[0, 0, 0]
-    start = (pos // TY * BE, pos % TY * BE)
-    win = window_of((x * mask).T, start)
-    maskf = mask.astype(jnp.float32)
-    tail = ((0, 0), (0, channels))
-    w_fwd = jnp.pad(weight.reshape(channels, 27 * channels), tail)
-    w_bwd = jnp.pad(weight.transpose(2, 1, 0).reshape(channels, 27 * channels), tail)
-    output, g, part = forward(win, w_fwd, cotangent[0, 0, 0], maskf)
-    total, x_grad = scattered(part, window_of(g.T, start), w_bwd, maskf)
+    mask = occupancy[0, 0].astype(jnp.float32)
+    channels = weight.shape[0]
+    w2 = weight.transpose(1, 0, 2).reshape(27 * channels, channels)
+    output, x_grad, total = fused(
+        features[0, 0, 0], cotangent[0, 0, 0], mask, coefficients(brick_pos[0, 0, 0]), w2
+    )
     mine = lax.dynamic_slice(total, (0, lax.axis_index("gy") % 2 * 6, 0), (2, 6, 16 * HALF))
     mine = mine.reshape(2, 6, HALF, 16)[:, :, :, :12].transpose(3, 0, 2, 1)
     w_grad = mine.reshape(12, 2 * HALF, 6)[:, :27] / (lax.axis_size("gx") * lax.axis_size("gy"))

time: 130 us -> 74.6 us (0.57)
  the two profiles are of different devices: /device:TPU:57 before, /device:TPU:17 now
where the time goes in v4:
time: 74.6 us; the launch traced here: 74.3 us
  Pallas kernels  65.8 us (88%)
  local copies, waits for them, and re-layouts  5.18 us (7%)
  other arithmetic  1.9 us (3%)
  between operations  1.38 us (2%)
    pallas_call x1, Pallas kernels, fused(): pl.pallas_call(fused_kernel, out_shape=(plane, plane, jax.ShapeDtypeStruc...  65.8 us
    unnamed x2, local copies, waits for them, and re-layouts  3.23 us

profile of v4, /device:TPU:17, one launch (start us, length us, event | category | flops | bytes accessed | tf_op | source)
XLA Modules:
  0.0 74.3 jit_solution(4908412097763382452)
XLA Ops:
  1.4 0.1 stack.67
  1.5 1.3 %convert_bitcast_fusion.mask = f32[1,512]{1,0:T(1,128)} fusion(s32[1,1,1,512]{3,2,1,0:T(1,128)} %param.6), kind=kLoop, calls=%fused_computation.2 | loop fusion | flops 512 | bytes 4096 | tf_op jit(solution)/shard_map/convert_element_type | solution.py:322
  2.7 0.7 broadcast_in_dim.12.coef
  3.4 65.8 %shard_map.76 = (bf16[192,512]{1,0:T(8,128)(2,1)}, bf16[192,512]{1,0:T(8,128)(2,1)}, f32[2,16,256]{2,1,0:T(8,128)}) custom-call(bf16[192,512]{1,0:T(8,128)(2,1)} %bitcast.39, bf16[192,512]{1,0:T(8,128)(2,1)} %bitcast.40, f32[1,512]{1,0:T(1,128)} %convert_bitcast_fusion.mask, f32[16,256]{1,0:T(8,128)} %broadcast_in_dim.12.coef, bf16[5184,192]{1,0:T(8,128)(2,1)} %bitcast.36), custom_call_target="tpu_custom_call" | custom-call | tf_op jit(solution)/shard_map/pallas_call | solution.py:270
  69.2 0.8 %constant_dynamic-slice_fusion = f32[2,6,224]{2,1,0:T(8,128)S(1)} fusion(f32[2,16,256]{2,1,0:T(8,128)} %get-tuple-element.8, s32[]{:T(128)S(6)} %select_n.21), kind=kLoop, calls=%fused_computation.3 | loop fusion | bytes 21508 | tf_op jit(solution)/shard_map/dynamic_slice | solution.py:328
  70.0 0.1 reshape.158
  70.1 0.2 copy.11
  70.3 0.1 reshape.159
  70.4 0.6 slice_multiply_fusion
  71.0 1.6 %copy.15 = bf16[1,1,1,192,512]{4,3,2,1,0:T(8,128)(2,1)} copy(bf16[1,1,1,192,512]{4,3,2,1,0:T(8,128)(2,1)} %bitcast.38) | data formatting | bytes 393216
  72.6 1.6 %copy.16 = bf16[1,1,1,192,512]{4,3,2,1,0:T(8,128)(2,1)} copy(bf16[1,1,1,192,512]{4,3,2,1,0:T(8,128)(2,1)} %bitcast.37) | data formatting | bytes 393216
  (3 shorter events, 0.0 us)

commit v5 on v4

--- a/solution.py
+++ b/solution.py
@@ -54,17 +54,17 @@
     for d, face in enumerate(faces):
         flat = face.reshape(64, 256)
         both = jnp.concatenate(
-            [flat * coef[2 * d : 2 * d + 1, :], flat * coef[2 * d + 1 : 2 * d + 2, :]], axis=0
+            [flat * coef[2 * d], flat * coef[2 * d + 1]], axis=0
         )
         face_tx[d] = both.astype(jnp.bfloat16)
     lines = (grid[7, 7], grid[7, 0], grid[0, 7], grid[0, 0])
     for d, line in enumerate(lines):
-        line = line * coef[8 + d : 9 + d, :]
+        line = line * coef[8 + d]
         line_tx[d] = jnp.concatenate([line, jnp.zeros_like(line)], axis=0).astype(jnp.bfloat16)
 
 
 def fill_ring(win, coef, face_rx, line_rx):
-    px0, px1, py0, py1 = (coef[12 + d : 13 + d, :] for d in range(4))
+    px0, px1, py0, py1 = coef[12:16]
     xm, xp, ym, yp = (
         face_rx[d].astype(jnp.float32).reshape(16, BE, 256) for d in range(4)
     )
@@ -84,14 +84,33 @@
     return jnp.concatenate([value, jnp.zeros((256 - channels, voxels), jnp.float32)], axis=0).T
 
 
+def coefficients(pos, gx, gy, nx, ny):
+    one = jnp.float32(1.0)
+    px, py = (pos >> 1).astype(jnp.float32), (pos & 1).astype(jnp.float32)
+    qx, qy = one - px, one - py
+    out_x = px * (gx < nx - 1).astype(jnp.float32)
+    in_x = qx * (gx > 0).astype(jnp.float32)
+    out_y = py * (gy < ny - 1).astype(jnp.float32)
+    in_y = qy * (gy > 0).astype(jnp.float32)
+    return (
+        out_x * qy, out_x * py, in_x * qy, in_x * py,
+        out_y * qx, out_y * px, in_y * qx, in_y * px,
+        out_x * out_y, out_x * in_y, in_x * out_y, in_x * in_y,
+        qx, px, qy, py,
+    )
+
+
 VMEM_SPEC = pl.BlockSpec(memory_space=pltpu.VMEM)
+HBM_SPEC = pl.BlockSpec(memory_space=pltpu.HBM)
+SMEM_SPEC = pl.BlockSpec(memory_space=pltpu.SMEM)
 
 
 def fused_kernel(
-    feat, cot, mask, coef, weight, output, x_grad, out, win, zs, odd, cols, packed, part,
+    feat, cot_hbm, mask, pos, weight_hbm, output_hbm, x_grad_hbm, out, cot, weight, output, x_grad,
+    local, win, zs, odd, cols, packed, part,
     face_tx, line_tx, face_rx, line_rx, core_rx, mid, x_rx, acc, yb, y_rx, flat, rows, turned,
     zb, z_rx, face_send, face_recv, line_send, line_recv,
-    core_send, core_recv, x_send, x_recv, y_send, y_recv, z_send, z_recv, fin_send, fin_recv,
+    relay, core_send, core_recv, x_send, x_recv, y_send, y_recv, z_send, z_recv, fin_send, fin_recv,
 ):
     gx, gy = lax.axis_index("gx"), lax.axis_index("gy")
     x, y = lax.div(gx, 4), lax.rem(gx, 4)
@@ -110,6 +129,14 @@
     gy_up, gy_down = lax.rem(gy + 1, ny), lax.rem(gy + ny - 1, ny)
     face_peer = [(gx_up, gy), (gx_down, gy), (gx, gy_up), (gx, gy_down)]
     line_peer = [(gx_up, gy_up), (gx_up, gy_down), (gx_down, gy_up), (gx_down, gy_down)]
+
+    load_weight = pltpu.make_async_copy(weight_hbm, weight, local.at[0])
+    load_cot = pltpu.make_async_copy(cot_hbm, cot, local.at[1])
+    save_output = pltpu.make_async_copy(output, output_hbm, local.at[2])
+    save_x_grad = pltpu.make_async_copy(x_grad, x_grad_hbm, local.at[3])
+    load_weight.start()
+    load_cot.start()
+    coef = coefficients(pos[0], gx, gy, nx, ny)
 
     barrier = pltpu.get_barrier_semaphore()
     peers = [partner] + x_peer[1:] + y_peer[1:] + q_peer[1:] + face_peer + line_peer
@@ -140,7 +167,7 @@
             )
         return copies
 
-    keep = mask[...]
+    keep = mask[...].astype(jnp.float32)
     bf, f32 = jnp.bfloat16, jnp.float32
     channels = feat.shape[0]
     x_halo, g_halo = halo(0), halo(1)
@@ -149,6 +176,7 @@
     for copy in x_halo:
         copy.start()
     win[1:9, 1:9] = own.reshape(BE, BE, BE, 256)
+    load_weight.wait()
     for pair in range(HALF):
         at = 2 * pair * channels
         left = weight[at : at + channels, :]
@@ -165,6 +193,8 @@
     pre = dot_nt(packed[...], cols[...])
     sigma = 1.0 / (1.0 + jnp.exp(-pre))
     output[...] = (pre * sigma * keep).astype(bf)
+    save_output.start()
+    load_cot.wait()
     slope = sigma * (1.0 + pre * (1.0 - sigma))
     g = (cot[...].astype(f32) * slope * keep).astype(bf)
     own = voxel_major(g.astype(f32))
@@ -190,33 +220,64 @@
     for k in order:
         core_copy[k].start()
     partial(core)
-    x_copy = {
-        k: remote(mid.at[x_of[k]], x_rx.at[k - 1], x_send.at[k - 1], x_recv.at[k - 1], x_peer[k])
-        for k in (2, 1, 3)
-    }
+    depth = part.shape[3]
+    cut = 1408
+    lanes_a, lanes_b = pl.ds(0, cut), pl.ds(cut, depth - cut)
+    far, right, left = x_of[2], x_of[1], x_of[3]
+    routes = (
+        (mid.at[far, :, lanes_a], relay.at[:, lanes_a], x_peer[1]),
+        (mid.at[far, :, lanes_b], relay.at[:, lanes_b], x_peer[3]),
+        (mid.at[right, :, lanes_b], x_rx.at[0, :, lanes_b], x_peer[1]),
+        (mid.at[left, :, lanes_a], x_rx.at[1, :, lanes_a], x_peer[3]),
+        (mid.at[right, :, lanes_a], x_rx.at[0, :, lanes_a], x_peer[1]),
+        (mid.at[left, :, lanes_b], x_rx.at[1, :, lanes_b], x_peer[3]),
+    )
+    x_copy = [
+        remote(src, dst, x_send.at[n], x_recv.at[n], peer)
+        for n, (src, dst, peer) in enumerate(routes)
+    ]
+
+    def pair_sum(d, lanes):
+        return part[core, d, :, lanes].astype(f32) + core_rx[d, :, lanes].astype(f32)
+
     acc[48:56, :] = jnp.zeros((8, acc.shape[1]), jnp.float32)
     rows[...] = jnp.zeros(rows.shape, jnp.float32)
     for k in order:
         core_copy[k].wait_recv()
-        total = part[core, x_of[k]].astype(jnp.float32) + core_rx[x_of[k]].astype(jnp.float32)
-        if k:
-            mid[x_of[k]] = total.astype(jnp.bfloat16)
-            x_copy[k].start()
+        if k == 2:
+            mid[far] = pair_sum(far, slice(None)).astype(bf)
+            x_copy[0].start()
+            x_copy[1].start()
+        elif k == 1:
+            mid[right, :, lanes_b] = pair_sum(right, lanes_b).astype(bf)
+            x_copy[2].start()
+        elif k == 3:
+            mid[left, :, lanes_a] = pair_sum(left, lanes_a).astype(bf)
+            x_copy[3].start()
         else:
-            acc[0:48, :] = total
+            acc[0:48, :] = pair_sum(x, slice(None))
     for copy in g_halo:
         copy.wait_recv()
     fill_ring(win, coef, face_rx.at[1], line_rx.at[1])
     shifted(win, zs, odd)
+    x_copy[0].wait_recv()
+    relayed = pair_sum(right, lanes_a) + relay[:, lanes_a].astype(f32)
+    mid[right, :, lanes_a] = relayed.astype(bf)
+    x_copy[4].start()
+    x_copy[1].wait_recv()
+    relayed = pair_sum(left, lanes_b) + relay[:, lanes_b].astype(f32)
+    mid[left, :, lanes_b] = relayed.astype(bf)
+    x_copy[5].start()
     fill_columns(cols, zs, odd, True)
     cut, end = 26 * channels, 27 * channels
     back = jnp.dot(cols[:, :cut], weight[:cut, :], preferred_element_type=f32)
     back = back + jnp.dot(cols[:, cut:end], weight[cut:end, :], preferred_element_type=f32)
     wide = jnp.concatenate([back, jnp.zeros((512, 256 - channels), f32)], axis=1)
     x_grad[...] = (wide.T[:channels] * keep).astype(bf)
-    for k in (1, 3, 2):
-        x_copy[k].wait_recv()
-        acc[0:48, :] += x_rx[k - 1].astype(jnp.float32)
+    save_x_grad.start()
+    for n in (2, 3, 4, 5):
+        x_copy[n].wait_recv()
+    acc[0:48, :] += x_rx[0].astype(f32) + x_rx[1].astype(f32)
     for j in range(4):
         yb[j] = acc[12 * j : 12 * j + 16, :].astype(jnp.bfloat16)
     y_copy = {
@@ -251,17 +312,20 @@
     last.start()
     for k in order:
         core_copy[k].wait_send()
+    for copy in x_copy:
+        copy.wait_send()
     for k in (2, 1, 3):
-        x_copy[k].wait_send()
         y_copy[k].wait_send()
     for copy in z_copy:
         copy.wait_send()
     for copy in x_halo + g_halo:
         copy.wait_send()
     last.wait()
-
-
-def fused(feat, cot, mask, coef, weight):
+    save_output.wait()
+    save_x_grad.wait()
+
+
+def fused(feat, cot, mask, pos, weight):
     channels, voxels = feat.shape
     depth = HALF * channels
     bf, f32 = jnp.bfloat16, jnp.float32
@@ -270,9 +334,14 @@
     return pl.pallas_call(
         fused_kernel,
         out_shape=(plane, plane, jax.ShapeDtypeStruct((2, 16, 256), f32)),
-        in_specs=[VMEM_SPEC] * 5,
-        out_specs=(VMEM_SPEC,) * 3,
+        in_specs=[VMEM_SPEC, HBM_SPEC, VMEM_SPEC, SMEM_SPEC, HBM_SPEC],
+        out_specs=(HBM_SPEC, HBM_SPEC, VMEM_SPEC),
         scratch_shapes=[
+            pltpu.VMEM((channels, voxels), bf),
+            pltpu.VMEM(weight.shape, bf),
+            pltpu.VMEM((channels, voxels), bf),
+            pltpu.VMEM((channels, voxels), bf),
+            dma((4,)),
             pltpu.VMEM((10, 10, BE, 256), f32),
             pltpu.VMEM((3, 10, 10, BE, 256), f32),
             pltpu.VMEM((3, 10, 10, BE, 256), f32),
@@ -285,7 +354,7 @@
             pltpu.VMEM((2, 4, 16, 256), bf),
             pltpu.VMEM((4, 48, depth), bf),
             pltpu.VMEM((4, 48, depth), bf),
-            pltpu.VMEM((3, 48, depth), bf),
+            pltpu.VMEM((2, 48, depth), bf),
             pltpu.VMEM((56, depth), f32),
             pltpu.VMEM((4, 16, depth), bf),
             pltpu.VMEM((3, 16, depth), bf),
@@ -295,35 +364,19 @@
             pltpu.VMEM((16, 16, 256), bf),
             pltpu.VMEM((15, 16, 256), bf),
             dma((2, 4)), dma((2, 4)), dma((2, 4)), dma((2, 4)),
-            dma((4,)), dma((4,)), dma((3,)), dma((3,)), dma((3,)), dma((3,)),
+            pltpu.VMEM((48, depth), bf),
+            dma((4,)), dma((4,)), dma((6,)), dma((6,)), dma((3,)), dma((3,)),
             dma((15,)), dma((15,)), dma, dma,
         ],
         compiler_params=pltpu.CompilerParams(collective_id=0, has_side_effects=True),
-    )(feat, cot, mask, coef, weight)
-
-
-def coefficients(pos):
-    gx, gy = lax.axis_index("gx"), lax.axis_index("gy")
-    px, py = pos // TY == 1, pos % TY == 1
-    up_x, up_y = gx < lax.axis_size("gx") - 1, gy < lax.axis_size("gy") - 1
-    down_x, down_y = gx > 0, gy > 0
-    out_x, in_x = px & up_x, ~px & down_x
-    out_y, in_y = py & up_y, ~py & down_y
-    flags = [
-        out_x & ~py, out_x & py, in_x & ~py, in_x & py,
-        out_y & ~px, out_y & px, in_y & ~px, in_y & px,
-        out_x & out_y, out_x & in_y, in_x & out_y, in_x & in_y,
-        ~px, px, ~py, py,
-    ]
-    return jnp.broadcast_to(jnp.stack(flags).astype(jnp.float32)[:, None], (16, 256))
+    )(feat, cot, mask, pos, weight)
 
 
 def shards(features, occupancy, brick_pos, weight, cotangent):
-    mask = occupancy[0, 0].astype(jnp.float32)
     channels = weight.shape[0]
     w2 = weight.transpose(1, 0, 2).reshape(27 * channels, channels)
     output, x_grad, total = fused(
-        features[0, 0, 0], cotangent[0, 0, 0], mask, coefficients(brick_pos[0, 0, 0]), w2
+        features[0, 0, 0], cotangent[0, 0, 0], occupancy[0, 0], brick_pos[0, 0], w2
     )
     mine = lax.dynamic_slice(total, (0, lax.axis_index("gy") % 2 * 6, 0), (2, 6, 16 * HALF))
     mine = mine.reshape(2, 6, HALF, 16)[:, :, :, :12].transpose(3, 0, 2, 1)

time: 74.6 us -> 69.3 us (0.929)
  the two profiles are of different devices: /device:TPU:17 before, /device:TPU:57 now
where the time goes in v5:
time: 69.3 us; the launch traced here: 68.6 us
  Pallas kernels  62.3 us (90%)
  local copies, waits for them, and re-layouts  4.39 us (6%)
  between operations  1.32 us (2%)
    pallas_call x1, Pallas kernels, fused(): pl.pallas_call(fused_kernel, out_shape=(plane, plane, jax.ShapeDtypeStruc...  62.3 us
    unnamed x2, local copies, waits for them, and re-layouts  3.23 us

profile of v5, /device:TPU:57, one launch (start us, length us, event | category | flops | bytes accessed | tf_op | source)
XLA Modules:
  0.0 68.6 jit_solution(4637521139674591091)
XLA Ops:
  1.3 62.3 %shard_map.76 = (bf16[192,512]{1,0:T(8,128)(2,1)}, bf16[192,512]{1,0:T(8,128)(2,1)}, f32[2,16,256]{2,1,0:T(8,128)}) custom-call(bf16[192,512]{1,0:T(8,128)(2,1)} %bitcast.17, bf16[192,512]{1,0:T(8,128)(2,1)} %bitcast.18, s32[1,512]{1,0:T(1,128)} %bitcast.21, s32[1]{0:T(128)} %bitcast.15.pos, bf16[5184,192]{1,0:T(8,128)(2,1)} %bitcast.16), custom_call_target="tpu_custom_call" | custom-call | tf_op jit(solution)/shard_map/pallas_call | solution.py:334
  63.6 0.8 %constant_dynamic-slice_fusion = f32[2,6,224]{2,1,0:T(8,128)S(1)} fusion(f32[2,16,256]{2,1,0:T(8,128)} %get-tuple-element.8, s32[]{:T(128)S(6)} %select_n.11), kind=kLoop, calls=%fused_computation.2 | loop fusion | bytes 21508 | tf_op jit(solution)/shard_map/dynamic_slice | solution.py:381
  64.3 0.1 reshape.16
  64.5 0.2 copy.11
  64.6 0.1 reshape.17
  64.7 0.6 slice_multiply_fusion
  65.4 1.6 %copy.15 = bf16[1,1,1,192,512]{4,3,2,1,0:T(8,128)(2,1)} copy(bf16[1,1,1,192,512]{4,3,2,1,0:T(8,128)(2,1)} %bitcast.20) | data formatting | bytes 393216
  67.0 1.6 %copy.16 = bf16[1,1,1,192,512]{4,3,2,1,0:T(8,128)(2,1)} copy(bf16[1,1,1,192,512]{4,3,2,1,0:T(8,128)(2,1)} %bitcast.19) | data formatting | bytes 393216
  (2 shorter events, 0.0 us)

commit v6 on v5

--- a/solution.py
+++ b/solution.py
@@ -197,11 +197,6 @@
     load_cot.wait()
     slope = sigma * (1.0 + pre * (1.0 - sigma))
     g = (cot[...].astype(f32) * slope * keep).astype(bf)
-    own = voxel_major(g.astype(f32))
-    halo_sends(own, coef, face_tx.at[1], line_tx.at[1])
-    for copy in g_halo:
-        copy.start()
-    win[1:9, 1:9] = own.reshape(BE, BE, BE, 256)
     depth = part.shape[3]
 
     def partial(half):
@@ -219,6 +214,11 @@
     }
     for k in order:
         core_copy[k].start()
+    own = voxel_major(g.astype(f32))
+    halo_sends(own, coef, face_tx.at[1], line_tx.at[1])
+    for copy in g_halo:
+        copy.start()
+    win[1:9, 1:9] = own.reshape(BE, BE, BE, 256)
     partial(core)
     depth = part.shape[3]
     cut = 1408
@@ -372,12 +372,37 @@
     )(feat, cot, mask, pos, weight)
 
 
+def finish_kernel(first, second, first_out, second_out, sems):
+    copies = [
+        pltpu.make_async_copy(first, first_out, sems.at[0]),
+        pltpu.make_async_copy(second, second_out, sems.at[1]),
+    ]
+    for copy in copies:
+        copy.start()
+    for copy in copies:
+        copy.wait()
+
+
+def finish(first, second):
+    return pl.pallas_call(
+        finish_kernel,
+        out_shape=(
+            jax.ShapeDtypeStruct(first.shape, first.dtype),
+            jax.ShapeDtypeStruct(second.shape, second.dtype),
+        ),
+        in_specs=[HBM_SPEC] * 2,
+        out_specs=(HBM_SPEC,) * 2,
+        scratch_shapes=[pltpu.SemaphoreType.DMA((2,))],
+    )(first, second)
+
+
 def shards(features, occupancy, brick_pos, weight, cotangent):
     channels = weight.shape[0]
     w2 = weight.transpose(1, 0, 2).reshape(27 * channels, channels)
     output, x_grad, total = fused(
         features[0, 0, 0], cotangent[0, 0, 0], occupancy[0, 0], brick_pos[0, 0], w2
     )
+    output, x_grad = finish(output, x_grad)
     mine = lax.dynamic_slice(total, (0, lax.axis_index("gy") % 2 * 6, 0), (2, 6, 16 * HALF))
     mine = mine.reshape(2, 6, HALF, 16)[:, :, :, :12].transpose(3, 0, 2, 1)
     w_grad = mine.reshape(12, 2 * HALF, 6)[:, :27] / (lax.axis_size("gx") * lax.axis_size("gy"))

time: 69.3 us -> 79.6 us (1.15)
  Pallas kernels: 62.3 us -> 75.9 us
  local copies, waits for them, and re-layouts: 4.39 us -> 1.16 us
    pallas_call x0 -> x1, Pallas kernels: none -> 13 us  [finish(): pl.pallas_call(finish_kernel, out_shape=(jax.ShapeDtypeStruct(first.shape...]
    unnamed x2 -> x0, local copies, waits for them, and re-layouts: 3.23 us -> none
where the time goes in v6:
time: 79.6 us; the launch traced here: 79 us
  Pallas kernels  75.9 us (95%)
  between operations  1.33 us (2%)
  local copies, waits for them, and re-layouts  1.16 us (1%)
    pallas_call x1, Pallas kernels, fused(): pl.pallas_call(fused_kernel, out_shape=(plane, plane, jax.ShapeDtypeStruc...  62.9 us
    pallas_call x1, Pallas kernels, finish(): pl.pallas_call(finish_kernel, out_shape=(jax.ShapeDtypeStruct(first.shape...  13 us

profile of v6, /device:TPU:57, one launch (start us, length us, event | category | flops | bytes accessed | tf_op | source)
XLA Modules:
  0.0 79.0 jit_solution(4148934519135019813)
XLA Ops:
  1.3 62.9 %shard_map.76 = (bf16[192,512]{1,0:T(8,128)(2,1)}, bf16[192,512]{1,0:T(8,128)(2,1)}, f32[2,16,256]{2,1,0:T(8,128)}) custom-call(bf16[192,512]{1,0:T(8,128)(2,1)} %bitcast.17, bf16[192,512]{1,0:T(8,128)(2,1)} %bitcast.18, s32[1,512]{1,0:T(1,128)} %bitcast.19, s32[1]{0:T(128)} %bitcast.15.pos, bf16[5184,192]{1,0:T(8,128)(2,1)} %bitcast.16), custom_call_target="tpu_custom_call" | custom-call | tf_op jit(solution)/shard_map/pallas_call | solution.py:334
  64.2 13.0 %shard_map.77 = (bf16[192,512]{1,0:T(8,128)(2,1)}, bf16[192,512]{1,0:T(8,128)(2,1)}) custom-call(bf16[192,512]{1,0:T(8,128)(2,1)} %get-tuple-element.8.first, bf16[192,512]{1,0:T(8,128)(2,1)} %get-tuple-element.9.second), custom_call_target="tpu_custom_call" | custom-call | tf_op jit(solution)/shard_map/pallas_call | solution.py:387
  77.2 0.8 constant_dynamic-slice_fusion
  78.0 0.1 reshape.16
  78.1 0.2 copy.11
  78.3 0.1 reshape.17
  78.4 0.6 slice_multiply_fusion
  (2 shorter events, 0.0 us)

commit v7 on v5

--- a/solution.py
+++ b/solution.py
@@ -372,12 +372,28 @@
     )(feat, cot, mask, pos, weight)
 
 
+def finish_kernel(first, second, first_out, second_out):
+    first_out[...] = first[...]
+    second_out[...] = second[...]
+
+
+def finish(first, second):
+    shape = jax.ShapeDtypeStruct(first.shape, first.dtype)
+    return pl.pallas_call(
+        finish_kernel,
+        out_shape=(shape, shape),
+        in_specs=[VMEM_SPEC] * 2,
+        out_specs=(VMEM_SPEC,) * 2,
+    )(first, second)
+
+
 def shards(features, occupancy, brick_pos, weight, cotangent):
     channels = weight.shape[0]
     w2 = weight.transpose(1, 0, 2).reshape(27 * channels, channels)
     output, x_grad, total = fused(
         features[0, 0, 0], cotangent[0, 0, 0], occupancy[0, 0], brick_pos[0, 0], w2
     )
+    output, x_grad = finish(output, x_grad)
     mine = lax.dynamic_slice(total, (0, lax.axis_index("gy") % 2 * 6, 0), (2, 6, 16 * HALF))
     mine = mine.reshape(2, 6, HALF, 16)[:, :, :, :12].transpose(3, 0, 2, 1)
     w_grad = mine.reshape(12, 2 * HALF, 6)[:, :27] / (lax.axis_size("gx") * lax.axis_size("gy"))

time: 69.3 us -> 67.8 us (0.978)
  local copies, waits for them, and re-layouts: 4.39 us -> 1.15 us
  Pallas kernels: 62.3 us -> 64 us
    unnamed x2 -> x0, local copies, waits for them, and re-layouts: 3.23 us -> none
    pallas_call x0 -> x1, Pallas kernels: none -> 1.78 us  [finish(): pl.pallas_call(finish_kernel, out_shape=(shape, shape), in_specs=[VMEM_SP...]
where the time goes in v7:
time: 67.8 us; the launch traced here: 67.1 us
  Pallas kernels  64 us (94%)
  between operations  1.3 us (2%)
  local copies, waits for them, and re-layouts  1.15 us (2%)
    pallas_call x1, Pallas kernels, fused(): pl.pallas_call(fused_kernel, out_shape=(plane, plane, jax.ShapeDtypeStruc...  62.2 us
    pallas_call x1, Pallas kernels, finish(): pl.pallas_call(finish_kernel, out_shape=(shape, shape), in_specs=[VMEM_SP...  1.78 us

profile of v7, /device:TPU:57, one launch (start us, length us, event | category | flops | bytes accessed | tf_op | source)
XLA Modules:
  0.0 67.1 jit_solution(1156219334726787968)
XLA Ops:
  1.3 62.2 %shard_map.76 = (bf16[192,512]{1,0:T(8,128)(2,1)}, bf16[192,512]{1,0:T(8,128)(2,1)}, f32[2,16,256]{2,1,0:T(8,128)}) custom-call(bf16[192,512]{1,0:T(8,128)(2,1)} %bitcast.17, bf16[192,512]{1,0:T(8,128)(2,1)} %bitcast.18, s32[1,512]{1,0:T(1,128)} %bitcast.19, s32[1]{0:T(128)} %bitcast.15.pos, bf16[5184,192]{1,0:T(8,128)(2,1)} %bitcast.16), custom_call_target="tpu_custom_call" | custom-call | tf_op jit(solution)/shard_map/pallas_call | solution.py:334
  63.5 1.8 %shard_map.77 = (bf16[192,512]{1,0:T(8,128)(2,1)}, bf16[192,512]{1,0:T(8,128)(2,1)}) custom-call(bf16[192,512]{1,0:T(8,128)(2,1)} %get-tuple-element.8.first, bf16[192,512]{1,0:T(8,128)(2,1)} %get-tuple-element.9.second), custom_call_target="tpu_custom_call" | custom-call | tf_op jit(solution)/shard_map/pallas_call | solution.py:382
  65.3 0.8 %constant_dynamic-slice_fusion = f32[2,6,224]{2,1,0:T(8,128)S(1)} fusion(f32[2,16,256]{2,1,0:T(8,128)} %get-tuple-element.12, s32[]{:T(128)S(6)} %select_n.11), kind=kLoop, calls=%fused_computation.2 | loop fusion | bytes 21508 | tf_op jit(solution)/shard_map/dynamic_slice | solution.py:397
  66.1 0.1 reshape.16
  66.2 0.2 copy.11
  66.4 0.1 reshape.17
  66.5 0.6 slice_multiply_fusion
  (2 shorter events, 0.0 us)
